TPU v7x, 512 devices: a whole 4x8x8 slice. The times are simulated.
512 devices in a mesh: tm: 128 (over z, y, core), zone: 4 (over x).
Axes of the slice: x: 4, y: 8, z: 8, core: 2. Of those that a mesh axis runs over, the one named last changes fastest.
Arguments:
- source_field: float32 [1024, 8192], P('tm', 'zone'), may hold values from -6 to 6
- remap_weights: bfloat16 [64, 8, 128, 128], P('zone'), may hold values from -0.1875 to 0.1875
- block_columns: int32 [64, 8], P('zone'), may hold values from 0 to 63, all different within a row
- piece_sizes: int32 [4, 128], P('zone'), may hold values from 1 to 64, 2048 in all within a row
- filter_taps: float32 [1023], replicated, may hold values from -0.1875 to 0.1875
Outputs:
- adjoint_field: float32 [1024, 8192], P('tm', 'zone')
Inputs may be any that keep to these rules, and one draw needn't show every extreme that they name: `block_columns`: the 8 source blocks of one target block are distinct; every source block feeds some target block. `piece_sizes`: each row sums to 2048; its largest basin has exactly 64 cells.
All inputs are finite; a program needn't handle non-finite values.
Results may differ from a plain program's by a relative error of at most 0.0038.
Values may be sent and summed in bfloat16 or wider, within the bound.
A program may use at most 64 MiB of HBM per device.

v0:
```python
import jax
import jax.numpy as jnp
from jax import lax
from jax.sharding import PartitionSpec as P


def toeplitz_rows(filter_taps, block_rows, span):
    tap_count = filter_taps.shape[0]
    extended = jnp.concatenate([filter_taps, jnp.zeros((span + 1 - tap_count,), filter_taps.dtype)])
    flat = jnp.broadcast_to(extended[None, :], (block_rows, span + 1)).reshape(
        block_rows * (span + 1)
    )
    return flat[: block_rows * span].reshape(block_rows, span)


def banded(series, filter_taps):
    length, breadth = series.shape
    tap_count = filter_taps.shape[0]
    half_width = (tap_count - 1) // 2
    block_rows = min(512, length)
    toeplitz = toeplitz_rows(filter_taps, block_rows, block_rows + 2 * half_width)
    padded = jnp.pad(series, ((half_width, half_width), (0, 0)))

    def one_block(start):
        window = lax.dynamic_slice_in_dim(padded, start, block_rows + 2 * half_width, 0)
        return jnp.dot(
            toeplitz, window, precision=lax.Precision.HIGHEST, preferred_element_type=jnp.float32
        )

    starts = jnp.arange(length // block_rows) * block_rows
    return lax.map(one_block, starts).reshape(length, breadth)


def relayout(sendbuf, filter_taps):
    received = lax.all_to_all(sendbuf, "tm", split_axis=1, concat_axis=0, tiled=True)
    total_rows, single, breadth = received.shape
    result = banded(received.reshape(total_rows, breadth), filter_taps).reshape(
        total_rows, single, breadth
    )
    return lax.all_to_all(
        result.astype(jnp.bfloat16), "tm", split_axis=0, concat_axis=1, tiled=True
    ).astype(result.dtype)


def shards(source_field, remap_weights, block_columns, piece_sizes, filter_taps):
    local_rows, zone_cells = source_field.shape
    owners = lax.axis_size("tm")
    block_size = remap_weights.shape[2]
    zone_blocks = remap_weights.shape[0]
    all_blocks = zone_blocks * lax.axis_size("zone")
    xlow = source_field.astype(jnp.bfloat16)
    xwhole = lax.all_gather(xlow, "zone", axis=1, tiled=True)
    picked = xwhole.reshape(local_rows, all_blocks, block_size)[:, block_columns]
    wind = jnp.einsum("tikb,ikab->tia", picked, remap_weights, preferred_element_type=jnp.float32)
    wind = wind.reshape(local_rows, zone_cells)
    stress = wind * jnp.abs(wind)
    sizes_row = piece_sizes[0]
    ends = jnp.cumsum(sizes_row)
    begins = ends - sizes_row
    cell_ids = jnp.arange(zone_cells, dtype=jnp.int32)
    member_mask = (cell_ids[:, None] >= begins[None, :]) & (cell_ids[:, None] < ends[None, :])
    member = member_mask.astype(jnp.float32)
    totals = jnp.dot(stress, member, precision=lax.Precision.HIGHEST)
    means = totals / sizes_row.astype(jnp.float32)[None, :]
    anomaly = stress - jnp.dot(means, member.T, precision=lax.Precision.HIGHEST)
    sendbuf = anomaly.reshape(local_rows, owners, zone_cells // owners)
    filtered = relayout(sendbuf, filter_taps).reshape(local_rows, zone_cells)
    flow_low = filtered.astype(jnp.bfloat16).reshape(local_rows, zone_blocks, block_size)
    contrib = jnp.einsum(
        "tia,ikab->tikb", flow_low, remap_weights, preferred_element_type=jnp.float32
    )
    partial_sum = jnp.zeros((local_rows, all_blocks, block_size), jnp.float32)
    partial_sum = partial_sum.at[:, block_columns].add(contrib)
    partial_sum = partial_sum.reshape(local_rows, all_blocks * block_size)
    return lax.psum_scatter(partial_sum, "zone", scatter_dimension=1, tiled=True)


def solution(mesh):
    return jax.shard_map(
        shards,
        mesh=mesh,
        in_specs=(
            P("tm", "zone"),
            P("zone", None, None, None),
            P("zone", None),
            P("zone", None),
            P(),
        ),
        out_specs=P("tm", "zone"),
        check_vma=False,
    )
```

profile of v0, /device:TPU:1, one launch (start us, length us, event | category | flops | bytes accessed | tf_op | source)
XLA Modules:
  0.0 141.8 jit_solution(17095864294425377096)
XLA Ops:
  6.5 0.8 copy.18
  7.6 0.7 convert_bitcast_fusion
  8.3 0.7 compare_select_fusion
  9.2 0.8 convert_element_type.29
  10.0 10.3 %all_gather.3 = bf16[8,8192]{1,0:T(8,128)(2,1)S(1)} all-gather(bf16[8,2048]{1,0:T(8,128)(2,1)S(1)} %convert_element_type.29), channel_id=1, replica_groups=mesh['tm'=128,'zone'=4] {'zone'}, dimensions={1}, use_global_device_ids=true | all-gather | bytes 163840 | tf_op jit(solution)/shard_map/all_gather | solution.py:52
  20.3 0.7 gather_fusion
  21.0 3.4 %abs_multiply_fusion = f32[8,2048]{1,0:T(8,128)S(1)} fusion(bf16[8,16,8,128]{3,0,2,1:T(8,128)(2,1)S(1)} %bitcast.72, bf16[16,8,128,128]{3,2,1,0:T(8,128)(2,1)} %param.8), kind=kOutput, calls=%fused_computation.17 | convolution fusion | flops 33587200 | bytes 4521984 | tf_op jit(solution)/shard_map/tikb,ikab->tia/dot_general | solution.py:54
  26.1 0.9 reshape.83
  26.9 20.5 %all-to-all-start = ((f32[128,1,128]{2,1,0:T(1,128)}), f32[128,1,128]{2,1,0:T(1,128)S(1)}, u32[]{:S(2)}, u32[]{:S(2)}) async-start(f32[128,1,128]{2,1,0:T(1,128)} %reshape.83), calls=%async_computation | async-start | bytes 131072 | tf_op jit(solution)/shard_map/all_to_all | solution.py:35
  48.1 3.8 %reshape.56 = f32[785920]{0:T(1024)} reshape(f32[512,1535]{1,0:T(8,128)S(1)} %broadcast_in_dim.15) | data formatting | bytes 6287360 | tf_op jit(solution)/shard_map/reshape | solution.py:10
  51.9 3.8 %slice.6 = f32[785408]{0:T(1024)} slice(f32[785920]{0:T(1024)} %reshape.56), slice={[0:785408]} | slice | bytes 6283264 | tf_op jit(solution)/shard_map/slice | solution.py:13
  55.7 4.1 %reshape.57 = f32[512,1534]{1,0:T(8,128)S(1)} reshape(f32[785408]{0:T(1024)} %slice.6) | data formatting | bytes 6283264 | tf_op jit(solution)/shard_map/reshape | solution.py:13
  60.3 0.8 reduce.2
  61.1 1.0 reshape.84
  62.1 1.9 %bitcast_bitcast_fusion = f32[1024,16]{1,0:T(8,128)} fusion(f32[128,8,16]{2,1,0:T(8,128)} %reshape.84), kind=kLoop, calls=%fused_computation.26 | loop fusion | bytes 131072 | tf_op jit(solution)/shard_map/reshape | solution.py:37
  64.0 1.2 copy.30
  65.3 10.5 %while.10 = (s32[]{:T(128)}, bf16[2,512,16]{1,2,0:T(8,128)(2,1)S(1)}, s32[2]{0:T(128)S(1)}, f32[2046,16]{0,1:T(8,128)S(1)}, f32[512,1534]{1,0:T(8,128)S(1)}, /*index=5*/s32[]{:T(128)}, s32[]{:T(128)}, s32[]{:T(128)}) while((s32[]{:T(128)}, bf16[2,512,16]{1,2,0:T(8,128)(2,1)S(1)}, s32[2]{0:T(128)S(1)}, f32[2046,16]{0,1:T(8,128)S(1)}, ...), condition=%wide.region_2.3_spmd, body=%wide.region_1.2_spmd.sunk | while | flops 150798336 | bytes 3276939 | solution.py:31
  67.8 2.7 %fusion.24 = bf16[2,512,16]{1,2,0:T(8,128)(2,1)S(1)} fusion(bf16[2,512,16]{1,2,0:T(8,128)(2,1)S(1)} %get-tuple-element.95, s32[]{:T(128)} %get-tuple-element.94, f32[512,1534]{1,0:T(8,128)S(1)} %get-tuple-element.106, f32[2046,16]{0,1:T(8,128)S(1)} %get-tuple-element.105, s32[]{:T(128)S(6)} %select_n.10), kind=kOutput, calls=%fused_computation.3.clone.1 | convolution fusion | flops 150798336 | bytes 3276808 | tf_op jit(solution)/shard_map/while/body/eval_jaxpr/dot_general | solution.py:26
  73.0 2.7 %fusion.24 = bf16[2,512,16]{1,2,0:T(8,128)(2,1)S(1)} fusion(bf16[2,512,16]{1,2,0:T(8,128)(2,1)S(1)} %get-tuple-element.95, s32[]{:T(128)} %get-tuple-element.94, f32[512,1534]{1,0:T(8,128)S(1)} %get-tuple-element.106, f32[2046,16]{0,1:T(8,128)S(1)} %get-tuple-element.105, s32[]{:T(128)S(6)} %select_n.10), kind=kOutput, calls=%fused_computation.3.clone.1 | convolution fusion | flops 150798336 | bytes 3276808 | tf_op jit(solution)/shard_map/while/body/eval_jaxpr/dot_general | solution.py:26
  76.2 34.1 %all_to_all.33 = bf16[1024,1,16]{2,1,0:T(2,128)(2,1)S(1)} all-to-all(bf16[1024,1,16]{2,1,0:T(2,128)(2,1)S(1)} %copy.22), channel_id=1, replica_groups=mesh['tm'=128,'zone'=4] {'tm'}, dimensions={0} | all-to-all | bytes 65536 | tf_op jit(solution)/shard_map/all_to_all | solution.py:40
  110.5 2.8 %fusion.10 = f32[16,8,8,128]{3,1,2,0:T(8,128)S(1)} fusion(bf16[16,8,128,128]{3,2,1,0:T(8,128)(2,1)} %param.8, bf16[8,16,128,1]{2,1,0,3:T(8,128)(2,1)S(1)} %bitcast.74), kind=kOutput, calls=%fused_computation.18 | convolution fusion | flops 33554432 | bytes 4751360 | tf_op jit(solution)/shard_map/tia,ikab->tikb/dot_general | solution.py:69
  113.4 4.9 %scatter_fusion = f32[8,64,128]{2,0,1:T(8,128)S(1)} fusion(f32[8,64,128]{2,0,1:T(8,128)S(1)} %broadcast_in_dim.11, s32[128]{0:T(128)S(1)} %reshape.69, f32[128,8,128]{2,1,0:T(8,128)S(1)} %bitcast.69), kind=kCustom, calls=%fused_computation.1 | custom fusion | flops 131072 | bytes 1573376 | tf_op jit(solution)/shard_map/scatter-add | solution.py:73
  118.4 0.7 copy-done
  119.1 15.9 %reduce-scatter.2.cloned.1.call-done = f32[8,2048]{1,0:T(8,128)} async-done(((f32[8,8192]{1,0:T(8,128)}), f32[8,2048]{1,0:T(8,128)}) %reduce-scatter.2.cloned.1.call-update) | async-done | bytes 65552 | tf_op jit(solution)/shard_map/reduce_scatter | solution.py:75
  (30 shorter events, 5.3 us)
Async XLA Ops:
  21.0 26.7 %copy-start.1 = (f32[1023]{0:T(1024)S(1)}, f32[1023]{0:T(1024)}, u32[]{:S(2)}) copy-start(f32[1023]{0:T(1024)} %param.11) | copy-start | bytes 12280
  26.9 32.8 %all-to-all-start = ((f32[128,1,128]{2,1,0:T(1,128)}), f32[128,1,128]{2,1,0:T(1,128)S(1)}, u32[]{:S(2)}, u32[]{:S(2)}) async-start(f32[128,1,128]{2,1,0:T(1,128)} %reshape.83), calls=%async_computation | async-start | bytes 131072 | tf_op jit(solution)/shard_map/all_to_all | solution.py:35
  47.4 87.5 %reduce-scatter.2.cloned.1.call-start = ((), (), s32[]{:S(2)}) async-start(), calls=%async_computation.3 | async-start | bytes 327680 | tf_op jit(solution)/shard_map/reduce_scatter | solution.py:75
  118.4 0.7 copy-start
Sparse Core Ops, SparseCore 0:
  119.2 15.6 reduce-scatter.1
where the time goes:
time: 144 us; the launch traced here: 142 us
  blocking collectives  44.3 us (31%)
  local copies, waits for them, and re-layouts  22.3 us (15%)
  starting transfers between devices  20.7 us (14%)
  waiting for transfers between devices  15.9 us (11%)
  between operations  13.6 us (9%)
  matrix products  12.8 us (9%)
  other arithmetic  8.3 us (6%)
  loops' own time  3.9 us (3%)
    all_to_all x1, blocking collectives, relayout(): lax.all_to_all(result.astype(jnp.bfloat16), 'tm', split_axis=0, concat_ax...  34.1 us
    all_to_all x1, starting transfers between devices, relayout(): lax.all_to_all(sendbuf, 'tm', split_axis=1, concat_axis=0, tiled=True)  20.5 us
    reduce_scatter x1, waiting for transfers between devices, shards(): lax.psum_scatter(partial_sum, 'zone', scatter_dimension=1, tiled=True)  15.9 us
    all_gather x1, blocking collectives, shards(): xwhole = lax.all_gather(xlow, 'zone', axis=1, tiled=True)  10.3 us
    dot_general x2, matrix products, one_block(): jnp.dot(toeplitz, window, precision=lax.Precision.HIGHEST, preferred_elem...  5.37 us
    scatter-add x1, other arithmetic, shards(): partial_sum = partial_sum.at[:, block_columns].add(contrib)  4.93 us
    reshape x1, local copies, waits for them, and re-layouts, toeplitz_rows(): return flat[:block_rows * span].reshape(block_rows, span)  4.06 us
    another operation x1, loops' own time, banded(): return lax.map(one_block, starts).reshape(length, breadth)  3.9 us
  transfers between devices with their start and end apart: 2, of which 1 were waited for; matrix products, arithmetic and copies ran while one was open for 9% of the time, Pallas kernels for 0%

commit v1 on v0

v1 whole, which is shorter than its diff:
```python
import functools

import jax
import jax.numpy as jnp
from jax import lax
from jax.experimental import pallas as pl
from jax.experimental.pallas import tpu as pltpu
from jax.sharding import PartitionSpec as P

MESH = pl.DeviceIdType.MESH
F32 = jnp.float32
BF16 = jnp.bfloat16
SNAP = 8
LANE = 128
BLOCKS = 16
SLOTS = 8
ROWS = 4


def iota(shape, dim):
    return lax.broadcasted_iota(jnp.int32, shape, dim)


def two_parts(value):
    high = value.astype(BF16)
    low = (value - high.astype(F32)).astype(BF16)
    return high, low


def ring_distance(offset, length):
    return min(offset, length - offset)


def plane_offsets(rings, ring, cores):
    span = ring * cores
    offsets = [(dz, dq) for dz in range(rings) for dq in range(span)]
    offsets.remove((0, 0))

    def hops(offset):
        dz, dq = offset
        return ring_distance(dz, rings) + ring_distance(dq // cores, ring)

    return sorted(offsets, key=lambda offset: -hops(offset))


def kernel(
    n_tm,
    n_zone,
    source,
    weights,
    columns,
    sizes,
    taps,
    out,
    x_in,
    x_all,
    w_all,
    cols,
    toeplitz,
    members,
    send_a,
    recv_a,
    send_b,
    recv_b,
    contrib,
    part_out,
    part_in,
    part_own,
    arranged,
    load_sem,
    x_send,
    x_recv,
    a_send,
    a_recv,
    b_send,
    b_recv,
    p_send,
    p_recv,
):
    tm = lax.axis_index("tm")
    zone = lax.axis_index("zone")
    rings, ring, cores = 8, 8, 2
    span = ring * cores
    tz, tq = tm // span, lax.rem(tm, span)
    others = []
    for dz, dq in plane_offsets(rings, ring, cores):
        others.append(lax.rem(tz + dz, rings) * span + lax.rem(tq + dq, span))
    zones = [lax.rem(zone + step, n_zone) for step in (2, 1, 3)]

    barrier = pltpu.get_barrier_semaphore()
    for peer in others:
        pl.semaphore_signal(barrier, inc=1, device_id={"tm": peer}, device_id_type=MESH)
    for peer in zones:
        pl.semaphore_signal(barrier, inc=1, device_id={"zone": peer}, device_id_type=MESH)

    load_x = pltpu.make_async_copy(source, x_in, load_sem.at[0])
    load_c = pltpu.make_async_copy(columns, cols, load_sem.at[1])
    load_w = pltpu.make_async_copy(weights, w_all, load_sem.at[2])
    load_x.start()
    load_c.start()
    load_w.start()

    tap_rows = taps[...]
    pieces = []
    for q in range(8):
        row = jnp.broadcast_to(tap_rows[q : q + 1, :], (8, LANE))
        pieces.append(jnp.where(lax.rem(iota((8, LANE), 1), 8) == iota((8, LANE), 0), row, 0.0))
    spread = jnp.concatenate(pieces, axis=1)
    pick = (iota((1024, LANE), 0) // 8 == iota((1024, LANE), 1)).astype(BF16)
    top, rest = two_parts(spread)
    last = (spread - top.astype(F32) - rest.astype(F32)).astype(BF16)
    by_phase = (
        jnp.dot(top, pick, preferred_element_type=F32)
        + jnp.dot(rest, pick, preferred_element_type=F32)
        + jnp.dot(last, pick, preferred_element_type=F32)
    )
    for n in range(15):
        phase, shift = (n, 63) if n < 8 else (n - 8, 64)
        line = jnp.concatenate([by_phase[phase : phase + 1, :], jnp.zeros((1, LANE), F32)], axis=1)
        wide = jnp.broadcast_to(line, (LANE, 2 * LANE))
        rolled = pltpu.roll(wide, 256 - shift, 1, stride=1, stride_axis=0)[:, :LANE]
        high, low = two_parts(rolled)
        toeplitz[n * LANE : (n + 1) * LANE, :LANE] = high
        toeplitz[n * LANE : (n + 1) * LANE, LANE:] = low

    size_row = sizes[...].astype(F32)
    size_wide = jnp.broadcast_to(size_row, (LANE, LANE))
    upto = jnp.sum(
        jnp.where(iota((LANE, LANE), 1) <= iota((LANE, LANE), 0), size_wide, 0.0), axis=1, keepdims=True
    )
    before = jnp.sum(
        jnp.where(iota((LANE, LANE), 1) < iota((LANE, LANE), 0), size_wide, 0.0), axis=1, keepdims=True
    )
    for i in range(BLOCKS):
        cell = (iota((LANE, LANE), 1) + i * LANE).astype(F32)
        inside = (cell >= before) & (cell < upto)
        members[:, i * LANE : (i + 1) * LANE] = inside.astype(BF16)

    load_x.wait()
    for i in range(BLOCKS):
        x_all[zone * BLOCKS + i] = x_in[:, i * LANE : (i + 1) * LANE].astype(BF16)
    pl.semaphore_wait(barrier, n_tm - 1 + n_zone - 1)
    mine = x_all.at[pl.ds(zone * BLOCKS, BLOCKS)]
    x_copies = []
    for n, peer in enumerate(zones):
        x_copies.append(
            pltpu.make_async_remote_copy(
                src_ref=mine,
                dst_ref=mine,
                send_sem=x_send.at[n],
                recv_sem=x_recv.at[n],
                device_id={"zone": peer},
                device_id_type=MESH,
            )
        )
        x_copies[-1].start()
    load_c.wait()
    load_w.wait()
    for copy in x_copies:
        copy.wait_recv()

    stress = []
    for i in range(BLOCKS):
        wind = jnp.zeros((SNAP, LANE), F32)
        for k in range(0, SLOTS, 2):
            x_pair = jnp.concatenate([x_all[cols[i, k]], x_all[cols[i, k + 1]]], axis=1)
            w_pair = jnp.concatenate([w_all[i, k], w_all[i, k + 1]], axis=1)
            wind += lax.dot_general(
                x_pair, w_pair, (((1,), (1,)), ((), ())), preferred_element_type=F32
            )
        stress.append(wind * jnp.abs(wind))

    wide = jnp.concatenate(stress, axis=1)
    high, low = two_parts(wide)
    member = members[...]
    both = jnp.concatenate([high, low], axis=0)
    totals = lax.dot_general(both, member, (((1,), (1,)), ((), ())), preferred_element_type=F32)
    means = (totals[:SNAP] + totals[SNAP:]) / size_row
    high, low = two_parts(means)
    both = jnp.concatenate([high, low], axis=0)
    spread = jnp.dot(both, member, preferred_element_type=F32)
    anomaly = wide - spread[:SNAP] - spread[SNAP:]
    tiles = jnp.concatenate([anomaly[:, i * LANE : (i + 1) * LANE] for i in range(BLOCKS)], axis=0)

    def exchange(send, recv, send_sem, recv_sem):
        recv[pl.ds(tm, 1)] = send[pl.ds(tm, 1)]
        for peer in others:
            pltpu.make_async_remote_copy(
                src_ref=send.at[pl.ds(peer, 1)],
                dst_ref=recv.at[pl.ds(tm, 1)],
                send_sem=send_sem,
                recv_sem=recv_sem,
                device_id={"tm": peer},
                device_id_type=MESH,
            ).start()

    def rows_wait(ref, sem):
        rows = ref.at[pl.ds(0, n_tm - 1)]
        pltpu.make_async_copy(rows, rows, sem).wait()

    send_a[...] = tiles.T.reshape(n_tm, 1, LANE)
    exchange(send_a, recv_a, a_send, a_recv)
    rows_wait(recv_a, a_recv)

    series = recv_a[...].reshape(n_tm, LANE)
    high, low = two_parts(series)
    upper = jnp.concatenate([high, low], axis=1)
    lower = jnp.concatenate([high, jnp.zeros_like(high)], axis=1)
    right = jnp.concatenate([upper, lower], axis=0)
    phase = lax.rem(iota((n_tm, LANE), 1), 8)
    filtered = jnp.zeros((n_tm, LANE), F32)
    for n in range(15):
        k = n - 7
        product = jnp.dot(toeplitz[n * LANE : (n + 1) * LANE, :], right, preferred_element_type=F32)
        product = product[:, :LANE] + product[:, LANE:]
        moved = product if k == 0 else pltpu.roll(product, (-k) % LANE, 1)
        filtered += jnp.where((phase + k >= 0) & (phase + k < 8), moved, 0.0)
    send_b[...] = filtered.reshape(n_tm, 1, LANE)
    exchange(send_b, recv_b, b_send, b_recv)
    rows_wait(recv_b, b_recv)

    flow = recv_b[...].reshape(n_tm, LANE).T.astype(BF16)
    for i in range(BLOCKS):
        left = flow[i * SNAP : (i + 1) * SNAP, :]
        for k in range(0, SLOTS, 2):
            w_pair = jnp.concatenate([w_all[i, k], w_all[i, k + 1]], axis=1)
            pair = jnp.dot(left, w_pair, preferred_element_type=F32)
            base = (i * SLOTS + k) * SNAP
            contrib[base : base + SNAP, :] = pair[:, :LANE]
            contrib[base + SNAP : base + 2 * SNAP, :] = pair[:, LANE:]
    n_pairs = BLOCKS * SLOTS
    all_blocks = BLOCKS * n_zone
    column_row = jnp.zeros((1, LANE), jnp.int32)
    lane = iota((1, LANE), 1)
    for i in range(BLOCKS):
        for k in range(SLOTS):
            column_row = jnp.where(lane == i * SLOTS + k, cols[i, k], column_row)
    chosen = (iota((all_blocks, LANE), 0) == column_row).astype(BF16)
    chosen = jnp.concatenate([chosen, chosen], axis=1)
    sums = []
    for t in range(0, SNAP, 2):
        sides = []
        for side in (t, t + 1):
            high, low = two_parts(contrib[pl.ds(side, n_pairs, stride=SNAP), :])
            sides.append(jnp.concatenate([high, low], axis=0))
        both = jnp.dot(chosen, jnp.concatenate(sides, axis=1), preferred_element_type=F32)
        sums += [both[:, :LANE], both[:, LANE:]]
    for t in range(SNAP):
        for z in range(n_zone):
            part = sums[t][z * BLOCKS : (z + 1) * BLOCKS]
            part_out[z, t] = part.astype(BF16)
            part_own[z, t] = part
    p_copies = []
    for n, peer in enumerate(zones):
        p_copies.append(
            pltpu.make_async_remote_copy(
                src_ref=part_out.at[peer],
                dst_ref=part_in.at[n],
                send_sem=p_send.at[n],
                recv_sem=p_recv.at[n],
                device_id={"zone": peer},
                device_id_type=MESH,
            )
        )
        p_copies[-1].start()
    for copy in p_copies:
        copy.wait_recv()
    for t in range(SNAP):
        total = part_own[zone, t]
        for n in range(n_zone - 1):
            total += part_in[n, t].astype(F32)
        arranged[pl.ds(t, BLOCKS, stride=SNAP), :] = total
    for i in range(BLOCKS):
        out[:, i * LANE : (i + 1) * LANE] = arranged[i * SNAP : (i + 1) * SNAP, :]
    for copy in x_copies + p_copies:
        copy.wait_send()
    rows_wait(send_a, a_send)
    rows_wait(send_b, b_send)


def solution(mesh):
    n_tm, n_zone = mesh.shape["tm"], mesh.shape["zone"]

    def shards(source_field, remap_weights, block_columns, piece_sizes, filter_taps):
        taps = jnp.pad(filter_taps, (0, 1)).reshape(8, LANE)
        any_space = pl.BlockSpec(memory_space=pl.ANY)
        vmem = pl.BlockSpec(memory_space=pltpu.VMEM)
        dma = pltpu.SemaphoreType.DMA
        return pl.pallas_call(
            functools.partial(kernel, n_tm, n_zone),
            name="flux",
            out_shape=jax.ShapeDtypeStruct(source_field.shape, F32),
            in_specs=[any_space, any_space, any_space, vmem, vmem],
            out_specs=vmem,
            scratch_shapes=[
                pltpu.VMEM(source_field.shape, F32),
                pltpu.VMEM((BLOCKS * n_zone, SNAP, LANE), BF16),
                pltpu.VMEM(remap_weights.shape, BF16),
                pltpu.SMEM(block_columns.shape, jnp.int32),
                pltpu.VMEM((15 * LANE, 2 * LANE), BF16),
                pltpu.VMEM((LANE, BLOCKS * LANE), BF16),
                pltpu.VMEM((n_tm, 1, LANE), F32),
                pltpu.VMEM((n_tm, 1, LANE), F32),
                pltpu.VMEM((n_tm, 1, LANE), F32),
                pltpu.VMEM((n_tm, 1, LANE), F32),
                pltpu.VMEM((BLOCKS * SLOTS * SNAP, LANE), F32),
                pltpu.VMEM((n_zone, SNAP, BLOCKS, LANE), BF16),
                pltpu.VMEM((n_zone - 1, SNAP, BLOCKS, LANE), BF16),
                pltpu.VMEM((n_zone, SNAP, BLOCKS, LANE), F32),
                pltpu.VMEM((BLOCKS * SNAP, LANE), F32),
                dma((3,)),
                dma((n_zone - 1,)),
                dma((n_zone - 1,)),
                dma,
                dma,
                dma,
                dma,
                dma((n_zone - 1,)),
                dma((n_zone - 1,)),
            ],
            compiler_params=pltpu.CompilerParams(collective_id=0, has_side_effects=True),
        )(source_field, remap_weights, block_columns, piece_sizes, taps)

    return jax.shard_map(
        shards,
        mesh=mesh,
        in_specs=(
            P("tm", "zone"),
            P("zone", None, None, None),
            P("zone", None),
            P("zone", None),
            P(),
        ),
        out_specs=P("tm", "zone"),
        check_vma=False,
    )
```

time: 144 us -> 46.9 us (0.33); the launches traced: 142 us -> 46.6 us
  blocking collectives: 44.3 us -> 0 us
  Pallas kernels: 0 us -> 42.5 us
  starting transfers between devices: 20.7 us -> 0 us
  local copies, waits for them, and re-layouts: 22.3 us -> 4.11 us
  waiting for transfers between devices: 15.9 us -> 0 us
  between operations: 13.6 us -> 0.01 us
  matrix products: 12.8 us -> 0 us
  other arithmetic: 8.3 us -> 0 us
  loops' own time: 3.9 us -> 0 us
    pallas_call x0 -> x1, Pallas kernels: none -> 42.5 us  [shards(): pl.pallas_call(functools.partial(kernel, n_tm, n_zone), name='flux', out_...]
    all_to_all x1 -> x0, blocking collectives: 34.1 us -> none  [relayout(): lax.all_to_all(result.astype(jnp.bfloat16), 'tm', split_axis=0, concat_ax...]
    all_to_all x1 -> x0, starting transfers between devices: 20.5 us -> none  [relayout(): lax.all_to_all(sendbuf, 'tm', split_axis=1, concat_axis=0, tiled=True)]
    reduce_scatter x1 -> x0, waiting for transfers between devices: 15.9 us -> none  [shards(): lax.psum_scatter(partial_sum, 'zone', scatter_dimension=1, tiled=True)]
    dot_general x6 -> x0, matrix products: 12.8 us -> none  [the longest x2 5.37 us: one_block(): jnp.dot(toeplitz, window, precision=lax.Precision.HIGHEST, preferred_elem...]
    all_gather x1 -> x0, blocking collectives: 10.3 us -> none  [shards(): xwhole = lax.all_gather(xlow, 'zone', axis=1, tiled=True)]
    reshape x6 -> x1, local copies, waits for them, and re-layouts: 11.1 us -> 1.28 us  [shards(): taps = jnp.pad(filter_taps, (0, 1)).reshape(8, LANE)]
    scatter-add x1 -> x0, other arithmetic: 4.93 us -> none  [shards(): partial_sum = partial_sum.at[:, block_columns].add(contrib)]
  transfers between devices with their start and end apart: 2 -> 0, of which waited for: 1 -> 0; matrix products, arithmetic and copies ran while one was open for 9% -> 0% of each run, Pallas kernels for 0% -> 0%
where the time goes in v1:
time: 46.9 us; the launch traced here: 46.6 us
  Pallas kernels  42.5 us (91%)
  local copies, waits for them, and re-layouts  4.11 us (9%)
    pallas_call x1, Pallas kernels, shards(): pl.pallas_call(functools.partial(kernel, n_tm, n_zone), name='flux', out_...  42.5 us
    unnamed x2, local copies, waits for them, and re-layouts  2.83 us
    reshape x1, local copies, waits for them, and re-layouts, shards(): taps = jnp.pad(filter_taps, (0, 1)).reshape(8, LANE)  1.28 us

profile of v1, /device:TPU:1, one launch (start us, length us, event | category | flops | bytes accessed | tf_op | source)
XLA Modules:
  0.0 46.6 jit_solution(12805370122028132777)
XLA Ops:
  0.0 1.3 %pad_bitcast_fusion.taps = f32[8,128]{1,0:T(8,128)} fusion(f32[1023]{0:T(1024)} %param.9), kind=kLoop, calls=%fused_computation | loop fusion | bytes 8188 | tf_op jit(solution)/shard_map/reshape | solution.py:285
  1.3 1.4 %copy.6.columns = s32[16,8]{1,0:T(8,128)} copy(s32[16,8]{0,1:T(8,128)} %param.7) | data formatting | bytes 1024 | tf_op args[2]
  2.6 42.5 %flux.1 = f32[8,2048]{1,0:T(8,128)} custom-call(f32[8,2048]{1,0:T(8,128)} %source.1, bf16[16,8,128,128]{3,2,1,0:T(8,128)(2,1)} %weights.1, s32[16,8]{1,0:T(8,128)} %copy.6.columns, s32[1,128]{1,0:T(1,128)} %sizes.1, f32[8,128]{1,0:T(8,128)} %pad_bitcast_fusion.taps), custom_call_target="tpu_custom_call" | custom-call | tf_op jit(solution)/shard_map/flux/pallas_call | solution.py:289
  45.1 1.5 %copy.8 = f32[8,2048]{1,0:T(8,128)} copy(f32[8,2048]{1,0:T(8,128)} %flux.1) | data formatting | bytes 131072

commit v2 on v1

--- a/solution.py
+++ b/solution.py
@@ -56,6 +56,8 @@
     x_all,
     w_all,
     cols,
+    size_in,
+    tap_in,
     toeplitz,
     members,
     send_a,
@@ -76,6 +78,7 @@
     b_recv,
     p_send,
     p_recv,
+    word,
 ):
     tm = lax.axis_index("tm")
     zone = lax.axis_index("zone")
@@ -87,59 +90,37 @@
         others.append(lax.rem(tz + dz, rings) * span + lax.rem(tq + dq, span))
     zones = [lax.rem(zone + step, n_zone) for step in (2, 1, 3)]
 
+    near, far_y, rows_near, far_z = [], [], [], []
+    for step in (2, 6, 1, 7):
+        side = lax.rem(tq + step * cores, span)
+        near += [tz * span + side, tz * span + side + 1 - 2 * lax.rem(side, cores)]
+        rows_near.append(lax.rem(tz + step, rings) * span + tq)
+        if step in (2, 6):
+            far_y.append(tz * span + side)
+            far_z.append(rows_near[-1])
+    near.append(tm + 1 - 2 * lax.rem(tm, cores))
+
+    def greet(semaphore, peers):
+        for peer in peers:
+            pl.semaphore_signal(semaphore, inc=1, device_id={"tm": peer}, device_id_type=MESH)
+
     barrier = pltpu.get_barrier_semaphore()
-    for peer in others:
-        pl.semaphore_signal(barrier, inc=1, device_id={"tm": peer}, device_id_type=MESH)
     for peer in zones:
         pl.semaphore_signal(barrier, inc=1, device_id={"zone": peer}, device_id_type=MESH)
+    greet(barrier, near + rows_near)
 
     load_x = pltpu.make_async_copy(source, x_in, load_sem.at[0])
     load_c = pltpu.make_async_copy(columns, cols, load_sem.at[1])
     load_w = pltpu.make_async_copy(weights, w_all, load_sem.at[2])
-    load_x.start()
-    load_c.start()
-    load_w.start()
-
-    tap_rows = taps[...]
-    pieces = []
-    for q in range(8):
-        row = jnp.broadcast_to(tap_rows[q : q + 1, :], (8, LANE))
-        pieces.append(jnp.where(lax.rem(iota((8, LANE), 1), 8) == iota((8, LANE), 0), row, 0.0))
-    spread = jnp.concatenate(pieces, axis=1)
-    pick = (iota((1024, LANE), 0) // 8 == iota((1024, LANE), 1)).astype(BF16)
-    top, rest = two_parts(spread)
-    last = (spread - top.astype(F32) - rest.astype(F32)).astype(BF16)
-    by_phase = (
-        jnp.dot(top, pick, preferred_element_type=F32)
-        + jnp.dot(rest, pick, preferred_element_type=F32)
-        + jnp.dot(last, pick, preferred_element_type=F32)
-    )
-    for n in range(15):
-        phase, shift = (n, 63) if n < 8 else (n - 8, 64)
-        line = jnp.concatenate([by_phase[phase : phase + 1, :], jnp.zeros((1, LANE), F32)], axis=1)
-        wide = jnp.broadcast_to(line, (LANE, 2 * LANE))
-        rolled = pltpu.roll(wide, 256 - shift, 1, stride=1, stride_axis=0)[:, :LANE]
-        high, low = two_parts(rolled)
-        toeplitz[n * LANE : (n + 1) * LANE, :LANE] = high
-        toeplitz[n * LANE : (n + 1) * LANE, LANE:] = low
-
-    size_row = sizes[...].astype(F32)
-    size_wide = jnp.broadcast_to(size_row, (LANE, LANE))
-    upto = jnp.sum(
-        jnp.where(iota((LANE, LANE), 1) <= iota((LANE, LANE), 0), size_wide, 0.0), axis=1, keepdims=True
-    )
-    before = jnp.sum(
-        jnp.where(iota((LANE, LANE), 1) < iota((LANE, LANE), 0), size_wide, 0.0), axis=1, keepdims=True
-    )
-    for i in range(BLOCKS):
-        cell = (iota((LANE, LANE), 1) + i * LANE).astype(F32)
-        inside = (cell >= before) & (cell < upto)
-        members[:, i * LANE : (i + 1) * LANE] = inside.astype(BF16)
+    load_s = pltpu.make_async_copy(sizes, size_in, load_sem.at[3])
+    load_t = pltpu.make_async_copy(taps, tap_in, load_sem.at[4])
+    for load in (load_x, load_c, load_s, load_w, load_t):
+        load.start()
 
     load_x.wait()
     for i in range(BLOCKS):
         x_all[zone * BLOCKS + i] = x_in[:, i * LANE : (i + 1) * LANE].astype(BF16)
-    pl.semaphore_wait(barrier, n_tm - 1 + n_zone - 1)
+    pl.semaphore_wait(barrier, n_zone - 1 + len(near) + len(rows_near))
     mine = x_all.at[pl.ds(zone * BLOCKS, BLOCKS)]
     x_copies = []
     for n, peer in enumerate(zones):
@@ -154,8 +135,28 @@
             )
         )
         x_copies[-1].start()
+    greet(word.at[0], far_y)
+
+    load_s.wait()
+    size_row = size_in[...].astype(F32)
+    size_wide = jnp.broadcast_to(size_row, (LANE, LANE))
+    upto = jnp.sum(
+        jnp.where(iota((LANE, LANE), 1) <= iota((LANE, LANE), 0), size_wide, 0.0), axis=1, keepdims=True
+    )
+    before = jnp.sum(
+        jnp.where(iota((LANE, LANE), 1) < iota((LANE, LANE), 0), size_wide, 0.0), axis=1, keepdims=True
+    )
+    for i in range(BLOCKS):
+        cell = (iota((LANE, LANE), 1) + i * LANE).astype(F32)
+        inside = (cell >= before) & (cell < upto)
+        members[:, i * LANE : (i + 1) * LANE] = inside.astype(BF16)
+
+    pl.semaphore_wait(word.at[0], len(far_y))
+    greet(word.at[1], rows_near)
     load_c.wait()
     load_w.wait()
+    pl.semaphore_wait(word.at[1], len(rows_near))
+    greet(word.at[2], far_z)
     for copy in x_copies:
         copy.wait_recv()
 
@@ -163,7 +164,7 @@
     for i in range(BLOCKS):
         wind = jnp.zeros((SNAP, LANE), F32)
         for k in range(0, SLOTS, 2):
-            x_pair = jnp.concatenate([x_all[cols[i, k]], x_all[cols[i, k + 1]]], axis=1)
+            x_pair = jnp.concatenate([x_all[cols[k, i]], x_all[cols[k + 1, i]]], axis=1)
             w_pair = jnp.concatenate([w_all[i, k], w_all[i, k + 1]], axis=1)
             wind += lax.dot_general(
                 x_pair, w_pair, (((1,), (1,)), ((), ())), preferred_element_type=F32
@@ -183,7 +184,6 @@
     tiles = jnp.concatenate([anomaly[:, i * LANE : (i + 1) * LANE] for i in range(BLOCKS)], axis=0)
 
     def exchange(send, recv, send_sem, recv_sem):
-        recv[pl.ds(tm, 1)] = send[pl.ds(tm, 1)]
         for peer in others:
             pltpu.make_async_remote_copy(
                 src_ref=send.at[pl.ds(peer, 1)],
@@ -193,13 +193,42 @@
                 device_id={"tm": peer},
                 device_id_type=MESH,
             ).start()
+        recv[pl.ds(tm, 1)] = send[pl.ds(tm, 1)]
 
     def rows_wait(ref, sem):
         rows = ref.at[pl.ds(0, n_tm - 1)]
         pltpu.make_async_copy(rows, rows, sem).wait()
 
     send_a[...] = tiles.T.reshape(n_tm, 1, LANE)
+    pl.semaphore_wait(word.at[2], len(far_z))
     exchange(send_a, recv_a, a_send, a_recv)
+
+    load_t.wait()
+    pieces = []
+    for q in range(8):
+        row = tap_in[pl.ds(q * LANE - q // 7, LANE)].reshape(1, LANE)
+        if q == 7:
+            row = jnp.where(iota((1, LANE), 1) < LANE - 1, pltpu.roll(row, LANE - 1, 1), 0.0)
+        row = jnp.broadcast_to(row, (8, LANE))
+        pieces.append(jnp.where(lax.rem(iota((8, LANE), 1), 8) == iota((8, LANE), 0), row, 0.0))
+    spread = jnp.concatenate(pieces, axis=1)
+    pick = (iota((1024, LANE), 0) // 8 == iota((1024, LANE), 1)).astype(BF16)
+    top, rest = two_parts(spread)
+    last = (spread - top.astype(F32) - rest.astype(F32)).astype(BF16)
+    by_phase = (
+        jnp.dot(top, pick, preferred_element_type=F32)
+        + jnp.dot(rest, pick, preferred_element_type=F32)
+        + jnp.dot(last, pick, preferred_element_type=F32)
+    )
+    for n in range(15):
+        phase, shift = (n, 63) if n < 8 else (n - 8, 64)
+        line = jnp.concatenate([by_phase[phase : phase + 1, :], jnp.zeros((1, LANE), F32)], axis=1)
+        turned = pltpu.roll(
+            jnp.broadcast_to(line, (LANE, 2 * LANE)), 256 - shift, 1, stride=1, stride_axis=0
+        )[:, :LANE]
+        high, low = two_parts(turned)
+        toeplitz[n * LANE : (n + 1) * LANE, :LANE] = high
+        toeplitz[n * LANE : (n + 1) * LANE, LANE:] = low
     rows_wait(recv_a, a_recv)
 
     series = recv_a[...].reshape(n_tm, LANE)
@@ -217,6 +246,16 @@
         filtered += jnp.where((phase + k >= 0) & (phase + k < 8), moved, 0.0)
     send_b[...] = filtered.reshape(n_tm, 1, LANE)
     exchange(send_b, recv_b, b_send, b_recv)
+
+    n_pairs = BLOCKS * SLOTS
+    all_blocks = BLOCKS * n_zone
+    column_row = jnp.zeros((1, LANE), jnp.int32)
+    lane = iota((1, LANE), 1)
+    for i in range(BLOCKS):
+        for k in range(SLOTS):
+            column_row = jnp.where(lane == i * SLOTS + k, cols[k, i], column_row)
+    chosen = (iota((all_blocks, LANE), 0) == column_row).astype(BF16)
+    chosen = jnp.concatenate([chosen, chosen], axis=1)
     rows_wait(recv_b, b_recv)
 
     flow = recv_b[...].reshape(n_tm, LANE).T.astype(BF16)
@@ -228,15 +267,6 @@
             base = (i * SLOTS + k) * SNAP
             contrib[base : base + SNAP, :] = pair[:, :LANE]
             contrib[base + SNAP : base + 2 * SNAP, :] = pair[:, LANE:]
-    n_pairs = BLOCKS * SLOTS
-    all_blocks = BLOCKS * n_zone
-    column_row = jnp.zeros((1, LANE), jnp.int32)
-    lane = iota((1, LANE), 1)
-    for i in range(BLOCKS):
-        for k in range(SLOTS):
-            column_row = jnp.where(lane == i * SLOTS + k, cols[i, k], column_row)
-    chosen = (iota((all_blocks, LANE), 0) == column_row).astype(BF16)
-    chosen = jnp.concatenate([chosen, chosen], axis=1)
     sums = []
     for t in range(0, SNAP, 2):
         sides = []
@@ -263,6 +293,10 @@
             )
         )
         p_copies[-1].start()
+    for copy in x_copies:
+        copy.wait_send()
+    rows_wait(send_a, a_send)
+    rows_wait(send_b, b_send)
     for copy in p_copies:
         copy.wait_recv()
     for t in range(SNAP):
@@ -272,31 +306,30 @@
         arranged[pl.ds(t, BLOCKS, stride=SNAP), :] = total
     for i in range(BLOCKS):
         out[:, i * LANE : (i + 1) * LANE] = arranged[i * SNAP : (i + 1) * SNAP, :]
-    for copy in x_copies + p_copies:
+    for copy in p_copies:
         copy.wait_send()
-    rows_wait(send_a, a_send)
-    rows_wait(send_b, b_send)
 
 
 def solution(mesh):
     n_tm, n_zone = mesh.shape["tm"], mesh.shape["zone"]
 
     def shards(source_field, remap_weights, block_columns, piece_sizes, filter_taps):
-        taps = jnp.pad(filter_taps, (0, 1)).reshape(8, LANE)
-        any_space = pl.BlockSpec(memory_space=pl.ANY)
+        hbm = pl.BlockSpec(memory_space=pltpu.HBM)
         vmem = pl.BlockSpec(memory_space=pltpu.VMEM)
         dma = pltpu.SemaphoreType.DMA
         return pl.pallas_call(
             functools.partial(kernel, n_tm, n_zone),
             name="flux",
             out_shape=jax.ShapeDtypeStruct(source_field.shape, F32),
-            in_specs=[any_space, any_space, any_space, vmem, vmem],
+            in_specs=[hbm] * 5,
             out_specs=vmem,
             scratch_shapes=[
                 pltpu.VMEM(source_field.shape, F32),
                 pltpu.VMEM((BLOCKS * n_zone, SNAP, LANE), BF16),
                 pltpu.VMEM(remap_weights.shape, BF16),
-                pltpu.SMEM(block_columns.shape, jnp.int32),
+                pltpu.SMEM((SLOTS, BLOCKS), jnp.int32),
+                pltpu.VMEM(piece_sizes.shape, jnp.int32),
+                pltpu.VMEM(filter_taps.shape, F32),
                 pltpu.VMEM((15 * LANE, 2 * LANE), BF16),
                 pltpu.VMEM((LANE, BLOCKS * LANE), BF16),
                 pltpu.VMEM((n_tm, 1, LANE), F32),
@@ -308,7 +341,7 @@
                 pltpu.VMEM((n_zone - 1, SNAP, BLOCKS, LANE), BF16),
                 pltpu.VMEM((n_zone, SNAP, BLOCKS, LANE), F32),
                 pltpu.VMEM((BLOCKS * SNAP, LANE), F32),
-                dma((3,)),
+                dma((5,)),
                 dma((n_zone - 1,)),
                 dma((n_zone - 1,)),
                 dma,
@@ -317,9 +350,10 @@
                 dma,
                 dma((n_zone - 1,)),
                 dma((n_zone - 1,)),
+                pltpu.SemaphoreType.REGULAR((3,)),
             ],
             compiler_params=pltpu.CompilerParams(collective_id=0, has_side_effects=True),
-        )(source_field, remap_weights, block_columns, piece_sizes, taps)
+        )(source_field, remap_weights, block_columns.T, piece_sizes, filter_taps)
 
     return jax.shard_map(
         shards,

time: 46.9 us -> 41.3 us (0.88)
  Pallas kernels: 42.5 us -> 39.7 us
  local copies, waits for them, and re-layouts: 4.11 us -> 1.47 us
    pallas_call x1, Pallas kernels: 42.5 us -> 39.7 us  [shards(): pl.pallas_call(functools.partial(kernel, n_tm, n_zone), name='flux', out_...]
    unnamed x2 -> x1, local copies, waits for them, and re-layouts: 2.83 us -> 1.47 us
    reshape x1 -> x0, local copies, waits for them, and re-layouts: 1.28 us -> none  [shards(): taps = jnp.pad(filter_taps, (0, 1)).reshape(8, LANE)]
where the time goes in v2:
time: 41.3 us; the launch traced here: 41.2 us
  Pallas kernels  39.7 us (96%)
  local copies, waits for them, and re-layouts  1.47 us (4%)
    pallas_call x1, Pallas kernels, shards(): pl.pallas_call(functools.partial(kernel, n_tm, n_zone), name='flux', out_...  39.7 us
    unnamed x1, local copies, waits for them, and re-layouts  1.47 us

profile of v2, /device:TPU:1, one launch (start us, length us, event | category | flops | bytes accessed | tf_op | source)
XLA Modules:
  0.0 41.2 jit_solution(16688845253234428909)
XLA Ops:
  0.0 39.7 %flux.1 = f32[8,2048]{1,0:T(8,128)} custom-call(f32[8,2048]{1,0:T(8,128)} %source.1, bf16[16,8,128,128]{3,2,1,0:T(8,128)(2,1)} %weights.1, s32[8,16]{1,0:T(8,128)} %bitcast.1, s32[1,128]{1,0:T(1,128)} %sizes.1, f32[1023]{0:T(1024)} %taps.1), custom_call_target="tpu_custom_call" | custom-call | tf_op jit(solution)/shard_map/flux/pallas_call | solution.py:320
  39.7 1.5 %copy.7 = f32[8,2048]{1,0:T(8,128)} copy(f32[8,2048]{1,0:T(8,128)} %flux.1) | data formatting | bytes 131072

commit v3 on v2

--- a/solution.py
+++ b/solution.py
@@ -14,7 +14,7 @@
 LANE = 128
 BLOCKS = 16
 SLOTS = 8
-ROWS = 4
+BANDS = [(0, 0), (0, 1)] + [(g, u) for g in (1, 2, 3) for u in (0, 1, 2)]
 
 
 def iota(shape, dim):
@@ -29,18 +29,6 @@
 
 def ring_distance(offset, length):
     return min(offset, length - offset)
-
-
-def plane_offsets(rings, ring, cores):
-    span = ring * cores
-    offsets = [(dz, dq) for dz in range(rings) for dq in range(span)]
-    offsets.remove((0, 0))
-
-    def hops(offset):
-        dz, dq = offset
-        return ring_distance(dz, rings) + ring_distance(dq // cores, ring)
-
-    return sorted(offsets, key=lambda offset: -hops(offset))
 
 
 def kernel(
@@ -78,36 +66,27 @@
     b_recv,
     p_send,
     p_recv,
-    word,
 ):
     tm = lax.axis_index("tm")
     zone = lax.axis_index("zone")
     rings, ring, cores = 8, 8, 2
     span = ring * cores
+    owners = n_tm // 2
     tz, tq = tm // span, lax.rem(tm, span)
-    others = []
-    for dz, dq in plane_offsets(rings, ring, cores):
-        others.append(lax.rem(tz + dz, rings) * span + lax.rem(tq + dq, span))
+    owner = tm < owners
+    sides = sorted(range(span), key=lambda dq: -ring_distance(dq // cores, ring))
     zones = [lax.rem(zone + step, n_zone) for step in (2, 1, 3)]
-
-    near, far_y, rows_near, far_z = [], [], [], []
-    for step in (2, 6, 1, 7):
-        side = lax.rem(tq + step * cores, span)
-        near += [tz * span + side, tz * span + side + 1 - 2 * lax.rem(side, cores)]
-        rows_near.append(lax.rem(tz + step, rings) * span + tq)
-        if step in (2, 6):
-            far_y.append(tz * span + side)
-            far_z.append(rows_near[-1])
-    near.append(tm + 1 - 2 * lax.rem(tm, cores))
-
-    def greet(semaphore, peers):
-        for peer in peers:
-            pl.semaphore_signal(semaphore, inc=1, device_id={"tm": peer}, device_id_type=MESH)
 
     barrier = pltpu.get_barrier_semaphore()
     for peer in zones:
         pl.semaphore_signal(barrier, inc=1, device_id={"zone": peer}, device_id_type=MESH)
-    greet(barrier, near + rows_near)
+
+    @pl.when(owner)
+    def _():
+        @pl.loop(1, n_tm)
+        def _(step):
+            peer = lax.rem(tm + step, n_tm)
+            pl.semaphore_signal(barrier, inc=1, device_id={"tm": peer}, device_id_type=MESH)
 
     load_x = pltpu.make_async_copy(source, x_in, load_sem.at[0])
     load_c = pltpu.make_async_copy(columns, cols, load_sem.at[1])
@@ -120,7 +99,7 @@
     load_x.wait()
     for i in range(BLOCKS):
         x_all[zone * BLOCKS + i] = x_in[:, i * LANE : (i + 1) * LANE].astype(BF16)
-    pl.semaphore_wait(barrier, n_zone - 1 + len(near) + len(rows_near))
+    pl.semaphore_wait(barrier, n_zone - 1 + owners - owner.astype(jnp.int32))
     mine = x_all.at[pl.ds(zone * BLOCKS, BLOCKS)]
     x_copies = []
     for n, peer in enumerate(zones):
@@ -135,7 +114,6 @@
             )
         )
         x_copies[-1].start()
-    greet(word.at[0], far_y)
 
     load_s.wait()
     size_row = size_in[...].astype(F32)
@@ -151,12 +129,9 @@
         inside = (cell >= before) & (cell < upto)
         members[:, i * LANE : (i + 1) * LANE] = inside.astype(BF16)
 
-    pl.semaphore_wait(word.at[0], len(far_y))
-    greet(word.at[1], rows_near)
+    load_t.wait()
     load_c.wait()
     load_w.wait()
-    pl.semaphore_wait(word.at[1], len(rows_near))
-    greet(word.at[2], far_z)
     for copy in x_copies:
         copy.wait_recv()
 
@@ -183,69 +158,114 @@
     anomaly = wide - spread[:SNAP] - spread[SNAP:]
     tiles = jnp.concatenate([anomaly[:, i * LANE : (i + 1) * LANE] for i in range(BLOCKS)], axis=0)
 
-    def exchange(send, recv, send_sem, recv_sem):
-        for peer in others:
-            pltpu.make_async_remote_copy(
-                src_ref=send.at[pl.ds(peer, 1)],
-                dst_ref=recv.at[pl.ds(tm, 1)],
-                send_sem=send_sem,
-                recv_sem=recv_sem,
-                device_id={"tm": peer},
-                device_id_type=MESH,
-            ).start()
-        recv[pl.ds(tm, 1)] = send[pl.ds(tm, 1)]
-
-    def rows_wait(ref, sem):
-        rows = ref.at[pl.ds(0, n_tm - 1)]
-        pltpu.make_async_copy(rows, rows, sem).wait()
-
-    send_a[...] = tiles.T.reshape(n_tm, 1, LANE)
-    pl.semaphore_wait(word.at[2], len(far_z))
-    exchange(send_a, recv_a, a_send, a_recv)
-
-    load_t.wait()
-    pieces = []
-    for q in range(8):
-        row = tap_in[pl.ds(q * LANE - q // 7, LANE)].reshape(1, LANE)
-        if q == 7:
-            row = jnp.where(iota((1, LANE), 1) < LANE - 1, pltpu.roll(row, LANE - 1, 1), 0.0)
-        row = jnp.broadcast_to(row, (8, LANE))
-        pieces.append(jnp.where(lax.rem(iota((8, LANE), 1), 8) == iota((8, LANE), 0), row, 0.0))
-    spread = jnp.concatenate(pieces, axis=1)
-    pick = (iota((1024, LANE), 0) // 8 == iota((1024, LANE), 1)).astype(BF16)
-    top, rest = two_parts(spread)
-    last = (spread - top.astype(F32) - rest.astype(F32)).astype(BF16)
-    by_phase = (
-        jnp.dot(top, pick, preferred_element_type=F32)
-        + jnp.dot(rest, pick, preferred_element_type=F32)
-        + jnp.dot(last, pick, preferred_element_type=F32)
-    )
-    for n in range(15):
-        phase, shift = (n, 63) if n < 8 else (n - 8, 64)
-        line = jnp.concatenate([by_phase[phase : phase + 1, :], jnp.zeros((1, LANE), F32)], axis=1)
-        turned = pltpu.roll(
-            jnp.broadcast_to(line, (LANE, 2 * LANE)), 256 - shift, 1, stride=1, stride_axis=0
-        )[:, :LANE]
-        high, low = two_parts(turned)
-        toeplitz[n * LANE : (n + 1) * LANE, :LANE] = high
-        toeplitz[n * LANE : (n + 1) * LANE, LANE:] = low
-    rows_wait(recv_a, a_recv)
-
-    series = recv_a[...].reshape(n_tm, LANE)
-    high, low = two_parts(series)
-    upper = jnp.concatenate([high, low], axis=1)
-    lower = jnp.concatenate([high, jnp.zeros_like(high)], axis=1)
-    right = jnp.concatenate([upper, lower], axis=0)
-    phase = lax.rem(iota((n_tm, LANE), 1), 8)
-    filtered = jnp.zeros((n_tm, LANE), F32)
-    for n in range(15):
-        k = n - 7
-        product = jnp.dot(toeplitz[n * LANE : (n + 1) * LANE, :], right, preferred_element_type=F32)
-        product = product[:, :LANE] + product[:, LANE:]
-        moved = product if k == 0 else pltpu.roll(product, (-k) % LANE, 1)
-        filtered += jnp.where((phase + k >= 0) & (phase + k < 8), moved, 0.0)
-    send_b[...] = filtered.reshape(n_tm, 1, LANE)
-    exchange(send_b, recv_b, b_send, b_recv)
+    def rows_wait(ref, rows, sem):
+        part = ref.at[pl.ds(0, rows)]
+        pltpu.make_async_copy(part, part, sem).wait()
+
+    def rows_wait_owners(ref, sem):
+        @pl.when(owner)
+        def _():
+            rows_wait(ref, 2 * owners - 2, sem)
+
+        @pl.when(jnp.logical_not(owner))
+        def _():
+            rows_wait(ref, 2 * owners, sem)
+
+    turned = tiles.T
+    first, second = turned[:owners], turned[owners:]
+    odd = lax.rem(iota((owners, LANE), 1) // 4, 2) == 1
+    send_a[pl.ds(0, owners, stride=2)] = jnp.where(odd, pltpu.roll(second, 4, 1), first).reshape(
+        owners, 1, LANE
+    )
+    send_a[pl.ds(1, owners, stride=2)] = jnp.where(odd, second, pltpu.roll(first, LANE - 4, 1)).reshape(
+        owners, 1, LANE
+    )
+
+    def send_row(peer):
+        pltpu.make_async_remote_copy(
+            src_ref=send_a.at[pl.ds(2 * peer, 2)],
+            dst_ref=recv_a.at[pl.ds(2 * tm, 2)],
+            send_sem=a_send,
+            recv_sem=a_recv,
+            device_id={"tm": peer},
+            device_id_type=MESH,
+        ).start()
+
+    steps = [(j, dq) for j in range(4) for dq in range(span)]
+    steps.sort(key=lambda step: -((4, 3, 2, 3)[step[0]] + ring_distance(step[1] // cores, ring)))
+    for j, dq in steps:
+        peer = lax.rem(tz + j, 4) * span + lax.rem(tq + dq, span)
+        if j == 0 and dq == 0:
+            pl.when(jnp.logical_not(owner))(functools.partial(send_row, peer))
+        else:
+            send_row(peer)
+
+    @pl.when(owner)
+    def _():
+        recv_a[pl.ds(2 * tm, 2)] = send_a[pl.ds(2 * tm, 2)]
+
+        pieces = []
+        for q in range(8):
+            row = tap_in[pl.ds(q * LANE - q // 7, LANE)].reshape(1, LANE)
+            if q == 7:
+                row = jnp.where(iota((1, LANE), 1) < LANE - 1, pltpu.roll(row, LANE - 1, 1), 0.0)
+            row = jnp.broadcast_to(row, (8, LANE))
+            pieces.append(jnp.where(lax.rem(iota((8, LANE), 1), 4) == iota((8, LANE), 0), row, 0.0))
+        spread = jnp.concatenate(pieces, axis=1)
+        pick = (iota((1024, 256), 0) // 4 == iota((1024, 256), 1)).astype(BF16)
+        top, rest = two_parts(spread)
+        last = (spread - top.astype(F32) - rest.astype(F32)).astype(BF16)
+        by_phase = (
+            jnp.dot(top, pick, preferred_element_type=F32)
+            + jnp.dot(rest, pick, preferred_element_type=F32)
+            + jnp.dot(last, pick, preferred_element_type=F32)
+        )
+        for n, (g, u) in enumerate(BANDS):
+            phase, start = (3, 127) if g == 0 else (g - 1, 128)
+            line = jnp.concatenate([by_phase[phase : phase + 1, :], jnp.zeros((1, 256), F32)], axis=1)
+            wide = jnp.broadcast_to(line, (LANE, 512))
+            high, low = two_parts(pltpu.roll(wide, (u - start) % 512, 1, stride=2, stride_axis=0)[:, :256])
+            for z in range(rings):
+                toeplitz[z, n * span : (n + 1) * span, :256] = high[z * span : (z + 1) * span]
+                toeplitz[z, n * span : (n + 1) * span, 256:] = low[z * span : (z + 1) * span]
+        rows_wait(recv_a, 2 * n_tm - 2, a_recv)
+
+        high, low = two_parts(recv_a[...].reshape(2 * n_tm, LANE))
+        upper = jnp.concatenate([high, low], axis=1)
+        lower = jnp.concatenate([high, jnp.zeros_like(high)], axis=1)
+        right = jnp.concatenate([upper, lower], axis=0)
+        place = lax.rem(iota((span, LANE), 1), 4)
+        for z in range(rings):
+            product = jnp.dot(toeplitz[z], right, preferred_element_type=F32)
+            product = product[:, :LANE] + product[:, LANE:]
+            band = {b: product[n * span : (n + 1) * span] for n, b in enumerate(BANDS)}
+            for u in range(2):
+                total = band[0, u]
+                for g in (1, 2, 3):
+                    total += jnp.where(
+                        place < 4 - g,
+                        pltpu.roll(band[g, u], LANE - g, 1),
+                        pltpu.roll(band[g, u + 1], 4 - g, 1),
+                    )
+                send_b[pl.ds(2 * z * span + u, span, stride=2)] = total.reshape(span, 1, LANE)
+
+            def send_back(peer):
+                pltpu.make_async_remote_copy(
+                    src_ref=send_b.at[pl.ds(2 * peer, 2)],
+                    dst_ref=recv_b.at[pl.ds(2 * tm, 2)],
+                    send_sem=b_send,
+                    recv_sem=b_recv,
+                    device_id={"tm": peer},
+                    device_id_type=MESH,
+                ).start()
+
+            for dq in sides:
+                peer = z * span + lax.rem(tq + dq, span)
+                if z < rings // 2 and dq == 0:
+                    pl.when(tz != z)(functools.partial(send_back, peer))
+                else:
+                    send_back(peer)
+        recv_b[pl.ds(2 * tm, 2)] = send_b[pl.ds(2 * tm, 2)]
 
     n_pairs = BLOCKS * SLOTS
     all_blocks = BLOCKS * n_zone
@@ -256,9 +276,13 @@
             column_row = jnp.where(lane == i * SLOTS + k, cols[k, i], column_row)
     chosen = (iota((all_blocks, LANE), 0) == column_row).astype(BF16)
     chosen = jnp.concatenate([chosen, chosen], axis=1)
-    rows_wait(recv_b, b_recv)
-
-    flow = recv_b[...].reshape(n_tm, LANE).T.astype(BF16)
+    rows_wait_owners(recv_b, b_recv)
+
+    even_row = recv_b[pl.ds(0, owners, stride=2)].reshape(owners, LANE)
+    odd_row = recv_b[pl.ds(1, owners, stride=2)].reshape(owners, LANE)
+    first = jnp.where(odd, pltpu.roll(odd_row, 4, 1), even_row)
+    second = jnp.where(odd, odd_row, pltpu.roll(even_row, LANE - 4, 1))
+    flow = jnp.concatenate([first, second], axis=0).T.astype(BF16)
     for i in range(BLOCKS):
         left = flow[i * SNAP : (i + 1) * SNAP, :]
         for k in range(0, SLOTS, 2):
@@ -295,8 +319,12 @@
         p_copies[-1].start()
     for copy in x_copies:
         copy.wait_send()
-    rows_wait(send_a, a_send)
-    rows_wait(send_b, b_send)
+    rows_wait_owners(send_a, a_send)
+
+    @pl.when(owner)
+    def _():
+        rows_wait(send_b, 2 * n_tm - 2, b_send)
+
     for copy in p_copies:
         copy.wait_recv()
     for t in range(SNAP):
@@ -320,7 +348,7 @@
         return pl.pallas_call(
             functools.partial(kernel, n_tm, n_zone),
             name="flux",
-            out_shape=jax.ShapeDtypeStruct(source_field.shape, F32),
+            out_shape=pltpu.VMEM(source_field.shape, F32),
             in_specs=[hbm] * 5,
             out_specs=vmem,
             scratch_shapes=[
@@ -330,11 +358,11 @@
                 pltpu.SMEM((SLOTS, BLOCKS), jnp.int32),
                 pltpu.VMEM(piece_sizes.shape, jnp.int32),
                 pltpu.VMEM(filter_taps.shape, F32),
-                pltpu.VMEM((15 * LANE, 2 * LANE), BF16),
+                pltpu.VMEM((8, len(BANDS) * 16, 512), BF16),
                 pltpu.VMEM((LANE, BLOCKS * LANE), BF16),
                 pltpu.VMEM((n_tm, 1, LANE), F32),
-                pltpu.VMEM((n_tm, 1, LANE), F32),
-                pltpu.VMEM((n_tm, 1, LANE), F32),
+                pltpu.VMEM((2 * n_tm, 1, LANE), F32),
+                pltpu.VMEM((2 * n_tm, 1, LANE), F32),
                 pltpu.VMEM((n_tm, 1, LANE), F32),
                 pltpu.VMEM((BLOCKS * SLOTS * SNAP, LANE), F32),
                 pltpu.VMEM((n_zone, SNAP, BLOCKS, LANE), BF16),
@@ -350,7 +378,6 @@
                 dma,
                 dma((n_zone - 1,)),
                 dma((n_zone - 1,)),
-                pltpu.SemaphoreType.REGULAR((3,)),
             ],
             compiler_params=pltpu.CompilerParams(collective_id=0, has_side_effects=True),
         )(source_field, remap_weights, block_columns.T, piece_sizes, filter_taps)

time: 41.3 us -> 39.8 us (0.964)
  local copies, waits for them, and re-layouts: 1.47 us -> 0.63 us
  Pallas kernels: 39.7 us -> 39.1 us
    unnamed x1, local copies, waits for them, and re-layouts: 1.47 us -> 0.63 us
    pallas_call x1, Pallas kernels: 39.7 us -> 39.1 us  [shards(): pl.pallas_call(functools.partial(kernel, n_tm, n_zone), name='flux', out_...]
where the time goes in v3:
time: 39.8 us; the launch traced here: 39.7 us
  Pallas kernels  39.1 us (98%)
  local copies, waits for them, and re-layouts  0.63 us (2%)
    pallas_call x1, Pallas kernels, shards(): pl.pallas_call(functools.partial(kernel, n_tm, n_zone), name='flux', out_...  39.1 us

profile of v3, /device:TPU:1, one launch (start us, length us, event | category | flops | bytes accessed | tf_op | source)
XLA Modules:
  0.0 39.7 jit_solution(12601884300664623432)
XLA Ops:
  0.0 39.1 %flux.1 = f32[8,2048]{1,0:T(8,128)S(1)} custom-call(f32[8,2048]{1,0:T(8,128)} %source.1, bf16[16,8,128,128]{3,2,1,0:T(8,128)(2,1)} %weights.1, s32[8,16]{1,0:T(8,128)} %bitcast.1, s32[1,128]{1,0:T(1,128)} %sizes.1, f32[1023]{0:T(1024)} %taps.1), custom_call_target="tpu_custom_call" | custom-call | tf_op jit(solution)/shard_map/flux/pallas_call | solution.py:348
  39.1 0.6 %copy.7 = f32[8,2048]{1,0:T(8,128)} copy(f32[8,2048]{1,0:T(8,128)S(1)} %flux.1) | data formatting | bytes 131072

commit v4 on v3

--- a/solution.py
+++ b/solution.py
@@ -14,6 +14,7 @@
 LANE = 128
 BLOCKS = 16
 SLOTS = 8
+SLABS = [(0, 1), (2, 3), (4, 5, 6, 7)]
 BANDS = [(0, 0), (0, 1)] + [(g, u) for g in (1, 2, 3) for u in (0, 1, 2)]
 
 
@@ -43,11 +44,13 @@
     x_in,
     x_all,
     w_all,
+    w_turned,
     cols,
     size_in,
     tap_in,
     toeplitz,
     members,
+    members_tall,
     send_a,
     recv_a,
     send_b,
@@ -66,6 +69,7 @@
     b_recv,
     p_send,
     p_recv,
+    word,
 ):
     tm = lax.axis_index("tm")
     zone = lax.axis_index("zone")
@@ -77,16 +81,35 @@
     sides = sorted(range(span), key=lambda dq: -ring_distance(dq // cores, ring))
     zones = [lax.rem(zone + step, n_zone) for step in (2, 1, 3)]
 
+    core = lax.rem(tq, cores)
+
+    def beside(step):
+        return tz * span + lax.rem(tq + step * cores + span, span)
+
+    def greet(semaphore, peer):
+        pl.semaphore_signal(semaphore, inc=1, device_id={"tm": peer}, device_id_type=MESH)
+
     barrier = pltpu.get_barrier_semaphore()
     for peer in zones:
         pl.semaphore_signal(barrier, inc=1, device_id={"zone": peer}, device_id_type=MESH)
-
-    @pl.when(owner)
-    def _():
-        @pl.loop(1, n_tm)
-        def _(step):
-            peer = lax.rem(tm + step, n_tm)
-            pl.semaphore_signal(barrier, inc=1, device_id={"tm": peer}, device_id_type=MESH)
+    lines = [lax.rem(tz + dz, 4) * span + tq for dz in (1, 2, 3)]
+    host = jnp.where(tz < 6, 3, 0) * span + tq
+    hosting = (tz == 0) | (tz == 3)
+    guests = [jnp.where(tz == 0, far, near) * span + tq for far, near in ((7, 4), (6, 5))]
+
+    @pl.when(owner)
+    def _():
+        for step in (2, -2, 1, -1):
+            greet(barrier, beside(step))
+            greet(barrier, beside(step) + 1 - 2 * core)
+        greet(barrier, tm + 1 - 2 * core)
+        for peer in lines:
+            greet(barrier, peer)
+
+    @pl.when(hosting)
+    def _():
+        for peer in guests:
+            greet(barrier, peer)
 
     load_x = pltpu.make_async_copy(source, x_in, load_sem.at[0])
     load_c = pltpu.make_async_copy(columns, cols, load_sem.at[1])
@@ -99,7 +122,7 @@
     load_x.wait()
     for i in range(BLOCKS):
         x_all[zone * BLOCKS + i] = x_in[:, i * LANE : (i + 1) * LANE].astype(BF16)
-    pl.semaphore_wait(barrier, n_zone - 1 + owners - owner.astype(jnp.int32))
+    pl.semaphore_wait(barrier, n_zone - 1 + jnp.where(owner, 12, 1))
     mine = x_all.at[pl.ds(zone * BLOCKS, BLOCKS)]
     x_copies = []
     for n, peer in enumerate(zones):
@@ -115,46 +138,61 @@
         )
         x_copies[-1].start()
 
+    @pl.when(owner)
+    def _():
+        for step in (2, -2):
+            greet(word.at[0], beside(step))
+
+    @pl.when(jnp.logical_not(owner))
+    def _():
+        greet(word.at[2], host)
+
     load_s.wait()
     size_row = size_in[...].astype(F32)
+    down, along = iota((LANE, LANE), 0), iota((LANE, LANE), 1)
     size_wide = jnp.broadcast_to(size_row, (LANE, LANE))
-    upto = jnp.sum(
-        jnp.where(iota((LANE, LANE), 1) <= iota((LANE, LANE), 0), size_wide, 0.0), axis=1, keepdims=True
-    )
-    before = jnp.sum(
-        jnp.where(iota((LANE, LANE), 1) < iota((LANE, LANE), 0), size_wide, 0.0), axis=1, keepdims=True
-    )
-    for i in range(BLOCKS):
-        cell = (iota((LANE, LANE), 1) + i * LANE).astype(F32)
+    size_tall = size_wide.T
+    upto = jnp.sum(jnp.where(along <= down, size_wide, 0.0), axis=1, keepdims=True)
+    before = jnp.sum(jnp.where(along < down, size_wide, 0.0), axis=1, keepdims=True)
+    upto_row = jnp.sum(jnp.where(down <= along, size_tall, 0.0), axis=0, keepdims=True)
+    before_row = jnp.sum(jnp.where(down < along, size_tall, 0.0), axis=0, keepdims=True)
+    for i in range(BLOCKS):
+        cell = (along + i * LANE).astype(F32)
         inside = (cell >= before) & (cell < upto)
         members[:, i * LANE : (i + 1) * LANE] = inside.astype(BF16)
+        cell = (down + i * LANE).astype(F32)
+        inside = (cell >= before_row) & (cell < upto_row)
+        members_tall[i * LANE : (i + 1) * LANE, :] = inside.astype(BF16)
+
+    @pl.when(owner)
+    def _():
+        pl.semaphore_wait(word.at[0], 2)
+        for peer in lines:
+            greet(word.at[1], peer)
 
     load_t.wait()
     load_c.wait()
     load_w.wait()
+    for i in range(BLOCKS):
+        for k in range(SLOTS):
+            w_turned[i, k * LANE : (k + 1) * LANE, :] = w_all[i, k].T
     for copy in x_copies:
         copy.wait_recv()
 
     stress = []
     for i in range(BLOCKS):
-        wind = jnp.zeros((SNAP, LANE), F32)
-        for k in range(0, SLOTS, 2):
-            x_pair = jnp.concatenate([x_all[cols[k, i]], x_all[cols[k + 1, i]]], axis=1)
-            w_pair = jnp.concatenate([w_all[i, k], w_all[i, k + 1]], axis=1)
-            wind += lax.dot_general(
-                x_pair, w_pair, (((1,), (1,)), ((), ())), preferred_element_type=F32
-            )
+        picked = jnp.concatenate([x_all[cols[k, i]] for k in range(SLOTS)], axis=1)
+        wind = jnp.dot(picked, w_turned[i], preferred_element_type=F32)
         stress.append(wind * jnp.abs(wind))
 
     wide = jnp.concatenate(stress, axis=1)
     high, low = two_parts(wide)
-    member = members[...]
     both = jnp.concatenate([high, low], axis=0)
-    totals = lax.dot_general(both, member, (((1,), (1,)), ((), ())), preferred_element_type=F32)
+    totals = jnp.dot(both, members_tall[...], preferred_element_type=F32)
     means = (totals[:SNAP] + totals[SNAP:]) / size_row
     high, low = two_parts(means)
     both = jnp.concatenate([high, low], axis=0)
-    spread = jnp.dot(both, member, preferred_element_type=F32)
+    spread = jnp.dot(both, members[...], preferred_element_type=F32)
     anomaly = wide - spread[:SNAP] - spread[SNAP:]
     tiles = jnp.concatenate([anomaly[:, i * LANE : (i + 1) * LANE] for i in range(BLOCKS)], axis=0)
 
@@ -193,12 +231,27 @@
 
     steps = [(j, dq) for j in range(4) for dq in range(span)]
     steps.sort(key=lambda step: -((4, 3, 2, 3)[step[0]] + ring_distance(step[1] // cores, ring)))
+
+    @pl.when(owner)
+    def _():
+        pl.semaphore_wait(word.at[1], 3)
+
+    @pl.when(jnp.logical_not(owner))
+    def _():
+        pl.semaphore_wait(word.at[3], 1)
+
     for j, dq in steps:
         peer = lax.rem(tz + j, 4) * span + lax.rem(tq + dq, span)
         if j == 0 and dq == 0:
             pl.when(jnp.logical_not(owner))(functools.partial(send_row, peer))
         else:
             send_row(peer)
+
+    @pl.when(hosting)
+    def _():
+        pl.semaphore_wait(word.at[2], 2)
+        for peer in guests:
+            greet(word.at[3], peer)
 
     @pl.when(owner)
     def _():
@@ -225,20 +278,33 @@
             line = jnp.concatenate([by_phase[phase : phase + 1, :], jnp.zeros((1, 256), F32)], axis=1)
             wide = jnp.broadcast_to(line, (LANE, 512))
             high, low = two_parts(pltpu.roll(wide, (u - start) % 512, 1, stride=2, stride_axis=0)[:, :256])
-            for z in range(rings):
-                toeplitz[z, n * span : (n + 1) * span, :256] = high[z * span : (z + 1) * span]
-                toeplitz[z, n * span : (n + 1) * span, 256:] = low[z * span : (z + 1) * span]
+            for slab, ref in zip(SLABS, toeplitz):
+                rows, base = len(slab) * span, slab[0] * span
+                ref[n * rows : (n + 1) * rows, :256] = high[base : base + rows]
+                ref[n * rows : (n + 1) * rows, 256:] = low[base : base + rows]
         rows_wait(recv_a, 2 * n_tm - 2, a_recv)
 
         high, low = two_parts(recv_a[...].reshape(2 * n_tm, LANE))
         upper = jnp.concatenate([high, low], axis=1)
         lower = jnp.concatenate([high, jnp.zeros_like(high)], axis=1)
         right = jnp.concatenate([upper, lower], axis=0)
-        place = lax.rem(iota((span, LANE), 1), 4)
-        for z in range(rings):
-            product = jnp.dot(toeplitz[z], right, preferred_element_type=F32)
+
+        def send_back(peer):
+            pltpu.make_async_remote_copy(
+                src_ref=send_b.at[pl.ds(2 * peer, 2)],
+                dst_ref=recv_b.at[pl.ds(2 * tm, 2)],
+                send_sem=b_send,
+                recv_sem=b_recv,
+                device_id={"tm": peer},
+                device_id_type=MESH,
+            ).start()
+
+        for slab, ref in zip(SLABS, toeplitz):
+            rows, base = len(slab) * span, slab[0] * span
+            place = lax.rem(iota((rows, LANE), 1), 4)
+            product = jnp.dot(ref[...], right, preferred_element_type=F32)
             product = product[:, :LANE] + product[:, LANE:]
-            band = {b: product[n * span : (n + 1) * span] for n, b in enumerate(BANDS)}
+            band = {b: product[n * rows : (n + 1) * rows] for n, b in enumerate(BANDS)}
             for u in range(2):
                 total = band[0, u]
                 for g in (1, 2, 3):
@@ -247,24 +313,14 @@
                         pltpu.roll(band[g, u], LANE - g, 1),
                         pltpu.roll(band[g, u + 1], 4 - g, 1),
                     )
-                send_b[pl.ds(2 * z * span + u, span, stride=2)] = total.reshape(span, 1, LANE)
-
-            def send_back(peer):
-                pltpu.make_async_remote_copy(
-                    src_ref=send_b.at[pl.ds(2 * peer, 2)],
-                    dst_ref=recv_b.at[pl.ds(2 * tm, 2)],
-                    send_sem=b_send,
-                    recv_sem=b_recv,
-                    device_id={"tm": peer},
-                    device_id_type=MESH,
-                ).start()
-
-            for dq in sides:
-                peer = z * span + lax.rem(tq + dq, span)
-                if z < rings // 2 and dq == 0:
-                    pl.when(tz != z)(functools.partial(send_back, peer))
-                else:
-                    send_back(peer)
+                send_b[pl.ds(2 * base + u, rows, stride=2)] = total.reshape(rows, 1, LANE)
+            for z in slab:
+                for dq in sides:
+                    peer = z * span + lax.rem(tq + dq, span)
+                    if z < rings // 2 and dq == 0:
+                        pl.when(tz != z)(functools.partial(send_back, peer))
+                    else:
+                        send_back(peer)
         recv_b[pl.ds(2 * tm, 2)] = send_b[pl.ds(2 * tm, 2)]
 
     n_pairs = BLOCKS * SLOTS
@@ -355,11 +411,13 @@
                 pltpu.VMEM(source_field.shape, F32),
                 pltpu.VMEM((BLOCKS * n_zone, SNAP, LANE), BF16),
                 pltpu.VMEM(remap_weights.shape, BF16),
+                pltpu.VMEM((BLOCKS, SLOTS * LANE, LANE), BF16),
                 pltpu.SMEM((SLOTS, BLOCKS), jnp.int32),
                 pltpu.VMEM(piece_sizes.shape, jnp.int32),
                 pltpu.VMEM(filter_taps.shape, F32),
-                pltpu.VMEM((8, len(BANDS) * 16, 512), BF16),
+                [pltpu.VMEM((len(BANDS) * len(slab) * 16, 512), BF16) for slab in SLABS],
                 pltpu.VMEM((LANE, BLOCKS * LANE), BF16),
+                pltpu.VMEM((BLOCKS * LANE, LANE), BF16),
                 pltpu.VMEM((n_tm, 1, LANE), F32),
                 pltpu.VMEM((2 * n_tm, 1, LANE), F32),
                 pltpu.VMEM((2 * n_tm, 1, LANE), F32),
@@ -378,6 +436,7 @@
                 dma,
                 dma((n_zone - 1,)),
                 dma((n_zone - 1,)),
+                pltpu.SemaphoreType.REGULAR((4,)),
             ],
             compiler_params=pltpu.CompilerParams(collective_id=0, has_side_effects=True),
         )(source_field, remap_weights, block_columns.T, piece_sizes, filter_taps)

time: 39.8 us -> 37.3 us (0.937)
  Pallas kernels: 39.1 us -> 36.6 us
    pallas_call x1, Pallas kernels: 39.1 us -> 36.6 us  [shards(): pl.pallas_call(functools.partial(kernel, n_tm, n_zone), name='flux', out_...]
where the time goes in v4:
time: 37.3 us; the launch traced here: 37.2 us
  Pallas kernels  36.6 us (98%)
  local copies, waits for them, and re-layouts  0.63 us (2%)
    pallas_call x1, Pallas kernels, shards(): pl.pallas_call(functools.partial(kernel, n_tm, n_zone), name='flux', out_...  36.6 us

profile of v4, /device:TPU:1, one launch (start us, length us, event | category | flops | bytes accessed | tf_op | source)
XLA Modules:
  0.0 37.2 jit_solution(1148974873461626966)
XLA Ops:
  0.0 36.6 %flux.1 = f32[8,2048]{1,0:T(8,128)S(1)} custom-call(f32[8,2048]{1,0:T(8,128)} %source.1, bf16[16,8,128,128]{3,2,1,0:T(8,128)(2,1)} %weights.1, s32[8,16]{1,0:T(8,128)} %bitcast.1, s32[1,128]{1,0:T(1,128)} %sizes.1, f32[1023]{0:T(1024)} %taps.1), custom_call_target="tpu_custom_call" | custom-call | tf_op jit(solution)/shard_map/flux/pallas_call | solution.py:404
  36.6 0.6 %copy.7 = f32[8,2048]{1,0:T(8,128)} copy(f32[8,2048]{1,0:T(8,128)S(1)} %flux.1) | data formatting | bytes 131072

commit v5 on v4

--- a/solution.py
+++ b/solution.py
@@ -55,6 +55,7 @@
     recv_a,
     send_b,
     recv_b,
+    paired,
     contrib,
     part_out,
     part_in,
@@ -89,6 +90,12 @@
     def greet(semaphore, peer):
         pl.semaphore_signal(semaphore, inc=1, device_id={"tm": peer}, device_id_type=MESH)
 
+    zone_order = [
+        jnp.where(zone == 2, 1, 2),
+        jnp.where((zone == 1) | (zone == 2), 3, 1),
+        jnp.where(zone == 0, 3, 0),
+    ]
+
     barrier = pltpu.get_barrier_semaphore()
     for peer in zones:
         pl.semaphore_signal(barrier, inc=1, device_id={"zone": peer}, device_id_type=MESH)
@@ -125,13 +132,14 @@
     pl.semaphore_wait(barrier, n_zone - 1 + jnp.where(owner, 12, 1))
     mine = x_all.at[pl.ds(zone * BLOCKS, BLOCKS)]
     x_copies = []
-    for n, peer in enumerate(zones):
+    for peer in zone_order:
+        step = lax.rem(peer - zone + n_zone, n_zone) - 1
         x_copies.append(
             pltpu.make_async_remote_copy(
                 src_ref=mine,
                 dst_ref=mine,
-                send_sem=x_send.at[n],
-                recv_sem=x_recv.at[n],
+                send_sem=x_send.at[step],
+                recv_sem=x_recv.at[step],
                 device_id={"zone": peer},
                 device_id_type=MESH,
             )
@@ -178,6 +186,16 @@
             w_turned[i, k * LANE : (k + 1) * LANE, :] = w_all[i, k].T
     for copy in x_copies:
         copy.wait_recv()
+
+    @pl.when(owner)
+    def _():
+        pl.semaphore_wait(word.at[1], 3)
+
+    @pl.when(hosting)
+    def _():
+        pl.semaphore_wait(word.at[2], 2)
+        for peer in guests:
+            greet(word.at[3], peer)
 
     stress = []
     for i in range(BLOCKS):
@@ -200,24 +218,20 @@
         part = ref.at[pl.ds(0, rows)]
         pltpu.make_async_copy(part, part, sem).wait()
 
-    def rows_wait_owners(ref, sem):
+    def rows_wait_owners(ref, each, sem):
         @pl.when(owner)
         def _():
-            rows_wait(ref, 2 * owners - 2, sem)
+            rows_wait(ref, each * (owners - 1), sem)
 
         @pl.when(jnp.logical_not(owner))
         def _():
-            rows_wait(ref, 2 * owners, sem)
+            rows_wait(ref, each * owners, sem)
 
     turned = tiles.T
     first, second = turned[:owners], turned[owners:]
     odd = lax.rem(iota((owners, LANE), 1) // 4, 2) == 1
-    send_a[pl.ds(0, owners, stride=2)] = jnp.where(odd, pltpu.roll(second, 4, 1), first).reshape(
-        owners, 1, LANE
-    )
-    send_a[pl.ds(1, owners, stride=2)] = jnp.where(odd, second, pltpu.roll(first, LANE - 4, 1)).reshape(
-        owners, 1, LANE
-    )
+    send_a[pl.ds(0, owners, stride=2), :] = jnp.where(odd, pltpu.roll(second, 4, 1), first)
+    send_a[pl.ds(1, owners, stride=2), :] = jnp.where(odd, second, pltpu.roll(first, LANE - 4, 1))
 
     def send_row(peer):
         pltpu.make_async_remote_copy(
@@ -232,10 +246,6 @@
     steps = [(j, dq) for j in range(4) for dq in range(span)]
     steps.sort(key=lambda step: -((4, 3, 2, 3)[step[0]] + ring_distance(step[1] // cores, ring)))
 
-    @pl.when(owner)
-    def _():
-        pl.semaphore_wait(word.at[1], 3)
-
     @pl.when(jnp.logical_not(owner))
     def _():
         pl.semaphore_wait(word.at[3], 1)
@@ -246,12 +256,6 @@
             pl.when(jnp.logical_not(owner))(functools.partial(send_row, peer))
         else:
             send_row(peer)
-
-    @pl.when(hosting)
-    def _():
-        pl.semaphore_wait(word.at[2], 2)
-        for peer in guests:
-            greet(word.at[3], peer)
 
     @pl.when(owner)
     def _():
@@ -284,7 +288,7 @@
                 ref[n * rows : (n + 1) * rows, 256:] = low[base : base + rows]
         rows_wait(recv_a, 2 * n_tm - 2, a_recv)
 
-        high, low = two_parts(recv_a[...].reshape(2 * n_tm, LANE))
+        high, low = two_parts(recv_a[...])
         upper = jnp.concatenate([high, low], axis=1)
         lower = jnp.concatenate([high, jnp.zeros_like(high)], axis=1)
         right = jnp.concatenate([upper, lower], axis=0)
@@ -313,7 +317,8 @@
                         pltpu.roll(band[g, u], LANE - g, 1),
                         pltpu.roll(band[g, u + 1], 4 - g, 1),
                     )
-                send_b[pl.ds(2 * base + u, rows, stride=2)] = total.reshape(rows, 1, LANE)
+                paired[pl.ds(2 * base + u, rows, stride=2), :] = total
+            send_b[2 * base : 2 * (base + rows), :] = paired[2 * base : 2 * (base + rows), :].astype(BF16)
             for z in slab:
                 for dq in sides:
                     peer = z * span + lax.rem(tq + dq, span)
@@ -321,7 +326,10 @@
                         pl.when(tz != z)(functools.partial(send_back, peer))
                     else:
                         send_back(peer)
-        recv_b[pl.ds(2 * tm, 2)] = send_b[pl.ds(2 * tm, 2)]
+        here = pl.ds(2 * tm, 2)
+        own = pltpu.make_async_copy(send_b.at[here], recv_b.at[here], load_sem.at[0])
+        own.start()
+        own.wait()
 
     n_pairs = BLOCKS * SLOTS
     all_blocks = BLOCKS * n_zone
@@ -332,10 +340,11 @@
             column_row = jnp.where(lane == i * SLOTS + k, cols[k, i], column_row)
     chosen = (iota((all_blocks, LANE), 0) == column_row).astype(BF16)
     chosen = jnp.concatenate([chosen, chosen], axis=1)
-    rows_wait_owners(recv_b, b_recv)
-
-    even_row = recv_b[pl.ds(0, owners, stride=2)].reshape(owners, LANE)
-    odd_row = recv_b[pl.ds(1, owners, stride=2)].reshape(owners, LANE)
+    rows_wait_owners(recv_b, 2, b_recv)
+
+    paired[: 2 * owners, :] = recv_b[...].astype(F32)
+    even_row = paired[pl.ds(0, owners, stride=2), :]
+    odd_row = paired[pl.ds(1, owners, stride=2), :]
     first = jnp.where(odd, pltpu.roll(odd_row, 4, 1), even_row)
     second = jnp.where(odd, odd_row, pltpu.roll(even_row, LANE - 4, 1))
     flow = jnp.concatenate([first, second], axis=0).T.astype(BF16)
@@ -375,7 +384,7 @@
         p_copies[-1].start()
     for copy in x_copies:
         copy.wait_send()
-    rows_wait_owners(send_a, a_send)
+    rows_wait_owners(send_a, 2, a_send)
 
     @pl.when(owner)
     def _():
@@ -418,10 +427,11 @@
                 [pltpu.VMEM((len(BANDS) * len(slab) * 16, 512), BF16) for slab in SLABS],
                 pltpu.VMEM((LANE, BLOCKS * LANE), BF16),
                 pltpu.VMEM((BLOCKS * LANE, LANE), BF16),
-                pltpu.VMEM((n_tm, 1, LANE), F32),
-                pltpu.VMEM((2 * n_tm, 1, LANE), F32),
-                pltpu.VMEM((2 * n_tm, 1, LANE), F32),
-                pltpu.VMEM((n_tm, 1, LANE), F32),
+                pltpu.VMEM((n_tm, LANE), F32),
+                pltpu.VMEM((2 * n_tm, LANE), F32),
+                pltpu.VMEM((2 * n_tm, LANE), BF16),
+                pltpu.VMEM((n_tm, LANE), BF16),
+                pltpu.VMEM((2 * n_tm, LANE), F32),
                 pltpu.VMEM((BLOCKS * SLOTS * SNAP, LANE), F32),
                 pltpu.VMEM((n_zone, SNAP, BLOCKS, LANE), BF16),
                 pltpu.VMEM((n_zone - 1, SNAP, BLOCKS, LANE), BF16),

time: 37.3 us -> 36 us (0.965)
  Pallas kernels: 36.6 us -> 35.3 us
    pallas_call x1, Pallas kernels: 36.6 us -> 35.3 us  [shards(): pl.pallas_call(functools.partial(kernel, n_tm, n_zone), name='flux', out_...]
where the time goes in v5:
time: 36 us; the launch traced here: 35.9 us
  Pallas kernels  35.3 us (98%)
  local copies, waits for them, and re-layouts  0.63 us (2%)
    pallas_call x1, Pallas kernels, shards(): pl.pallas_call(functools.partial(kernel, n_tm, n_zone), name='flux', out_...  35.3 us

profile of v5, /device:TPU:1, one launch (start us, length us, event | category | flops | bytes accessed | tf_op | source)
XLA Modules:
  0.0 35.9 jit_solution(12839580348438738053)
XLA Ops:
  0.0 35.3 %flux.1 = f32[8,2048]{1,0:T(8,128)S(1)} custom-call(f32[8,2048]{1,0:T(8,128)} %source.1, bf16[16,8,128,128]{3,2,1,0:T(8,128)(2,1)} %weights.1, s32[8,16]{1,0:T(8,128)} %bitcast.1, s32[1,128]{1,0:T(1,128)} %sizes.1, f32[1023]{0:T(1024)} %taps.1), custom_call_target="tpu_custom_call" | custom-call | tf_op jit(solution)/shard_map/flux/pallas_call | solution.py:413
  35.3 0.6 %copy.7 = f32[8,2048]{1,0:T(8,128)} copy(f32[8,2048]{1,0:T(8,128)S(1)} %flux.1) | data formatting | bytes 131072

commit v6 on v5

--- a/solution.py
+++ b/solution.py
@@ -218,14 +218,14 @@
         part = ref.at[pl.ds(0, rows)]
         pltpu.make_async_copy(part, part, sem).wait()
 
-    def rows_wait_owners(ref, each, sem):
+    def rows_wait_owners(ref, sem):
         @pl.when(owner)
         def _():
-            rows_wait(ref, each * (owners - 1), sem)
+            rows_wait(ref, 2 * owners - 2, sem)
 
         @pl.when(jnp.logical_not(owner))
         def _():
-            rows_wait(ref, each * owners, sem)
+            rows_wait(ref, 2 * owners, sem)
 
     turned = tiles.T
     first, second = turned[:owners], turned[owners:]
@@ -298,7 +298,7 @@
                 src_ref=send_b.at[pl.ds(2 * peer, 2)],
                 dst_ref=recv_b.at[pl.ds(2 * tm, 2)],
                 send_sem=b_send,
-                recv_sem=b_recv,
+                recv_sem=b_recv.at[tz // 2],
                 device_id={"tm": peer},
                 device_id_type=MESH,
             ).start()
@@ -340,22 +340,45 @@
             column_row = jnp.where(lane == i * SLOTS + k, cols[k, i], column_row)
     chosen = (iota((all_blocks, LANE), 0) == column_row).astype(BF16)
     chosen = jnp.concatenate([chosen, chosen], axis=1)
-    rows_wait_owners(recv_b, 2, b_recv)
-
-    paired[: 2 * owners, :] = recv_b[...].astype(F32)
-    even_row = paired[pl.ds(0, owners, stride=2), :]
-    odd_row = paired[pl.ds(1, owners, stride=2), :]
-    first = jnp.where(odd, pltpu.roll(odd_row, 4, 1), even_row)
-    second = jnp.where(odd, odd_row, pltpu.roll(even_row, LANE - 4, 1))
-    flow = jnp.concatenate([first, second], axis=0).T.astype(BF16)
-    for i in range(BLOCKS):
-        left = flow[i * SNAP : (i + 1) * SNAP, :]
-        for k in range(0, SLOTS, 2):
-            w_pair = jnp.concatenate([w_all[i, k], w_all[i, k + 1]], axis=1)
-            pair = jnp.dot(left, w_pair, preferred_element_type=F32)
-            base = (i * SLOTS + k) * SNAP
-            contrib[base : base + SNAP, :] = pair[:, :LANE]
-            contrib[base + SNAP : base + 2 * SNAP, :] = pair[:, LANE:]
+
+    quarter = owners // 2
+    odd = lax.rem(iota((quarter, LANE), 1) // 4, 2) == 1
+    for part in range(2):
+        mine_too = owner & (tz // 2 == part)
+        from_rows = recv_b.at[pl.ds(owners * part, owners)]
+        but_mine = recv_b.at[pl.ds(owners * part, owners - 2)]
+
+        @pl.when(mine_too)
+        def _():
+            pltpu.make_async_copy(but_mine, but_mine, b_recv.at[part]).wait()
+
+        @pl.when(jnp.logical_not(mine_too))
+        def _():
+            pltpu.make_async_copy(from_rows, from_rows, b_recv.at[part]).wait()
+
+        paired[part * owners : (part + 1) * owners, :] = recv_b[part * owners : (part + 1) * owners, :].astype(F32)
+        even_row = paired[pl.ds(part * owners, quarter, stride=2), :]
+        odd_row = paired[pl.ds(part * owners + 1, quarter, stride=2), :]
+        first = jnp.where(odd, pltpu.roll(odd_row, 4, 1), even_row)
+        second = jnp.where(odd, odd_row, pltpu.roll(even_row, LANE - 4, 1))
+        flow = jnp.concatenate([first, second], axis=0).T.astype(BF16)
+        low_a, high_a = part * quarter, owners + part * quarter
+        for i in range(BLOCKS):
+            left = flow[i * SNAP : (i + 1) * SNAP, :]
+            for k in range(0, SLOTS, 2):
+                w_low = [w_all[i, n, low_a : low_a + quarter, :] for n in (k, k + 1)]
+                w_high = [w_all[i, n, high_a : high_a + quarter, :] for n in (k, k + 1)]
+                w_pair = jnp.concatenate(
+                    [jnp.concatenate(w_low, axis=1), jnp.concatenate(w_high, axis=1)], axis=0
+                )
+                pair = jnp.dot(left, w_pair, preferred_element_type=F32)
+                for n in range(2):
+                    base = (i * SLOTS + k + n) * SNAP
+                    term = pair[:, n * LANE : (n + 1) * LANE]
+                    if part == 0:
+                        contrib[base : base + SNAP, :] = term
+                    else:
+                        contrib[base : base + SNAP, :] += term
     sums = []
     for t in range(0, SNAP, 2):
         sides = []
@@ -384,7 +407,7 @@
         p_copies[-1].start()
     for copy in x_copies:
         copy.wait_send()
-    rows_wait_owners(send_a, 2, a_send)
+    rows_wait_owners(send_a, a_send)
 
     @pl.when(owner)
     def _():
@@ -443,7 +466,7 @@
                 dma,
                 dma,
                 dma,
-                dma,
+                dma((2,)),
                 dma((n_zone - 1,)),
                 dma((n_zone - 1,)),
                 pltpu.SemaphoreType.REGULAR((4,)),

time: 36 us -> 35.8 us (level)
  no operation moved by 1% of the time
where the time goes in v6:
time: 35.8 us; the launch traced here: 35.7 us
  Pallas kernels  35 us (98%)
  local copies, waits for them, and re-layouts  0.63 us (2%)
    pallas_call x1, Pallas kernels, shards(): pl.pallas_call(functools.partial(kernel, n_tm, n_zone), name='flux', out_...  35 us

profile of v6, /device:TPU:1, one launch (start us, length us, event | category | flops | bytes accessed | tf_op | source)
XLA Modules:
  0.0 35.7 jit_solution(15539026933270844225)
XLA Ops:
  0.0 35.0 %flux.1 = f32[8,2048]{1,0:T(8,128)S(1)} custom-call(f32[8,2048]{1,0:T(8,128)} %source.1, bf16[16,8,128,128]{3,2,1,0:T(8,128)(2,1)} %weights.1, s32[8,16]{1,0:T(8,128)} %bitcast.1, s32[1,128]{1,0:T(1,128)} %sizes.1, f32[1023]{0:T(1024)} %taps.1), custom_call_target="tpu_custom_call" | custom-call | tf_op jit(solution)/shard_map/flux/pallas_call | solution.py:436
  35.0 0.6 %copy.7 = f32[8,2048]{1,0:T(8,128)} copy(f32[8,2048]{1,0:T(8,128)S(1)} %flux.1) | data formatting | bytes 131072

commit v7 on v6

--- a/solution.py
+++ b/solution.py
@@ -298,7 +298,7 @@
                 src_ref=send_b.at[pl.ds(2 * peer, 2)],
                 dst_ref=recv_b.at[pl.ds(2 * tm, 2)],
                 send_sem=b_send,
-                recv_sem=b_recv.at[tz // 2],
+                recv_sem=b_recv.at[tz],
                 device_id={"tm": peer},
                 device_id_type=MESH,
             ).start()
@@ -341,12 +341,13 @@
     chosen = (iota((all_blocks, LANE), 0) == column_row).astype(BF16)
     chosen = jnp.concatenate([chosen, chosen], axis=1)
 
-    quarter = owners // 2
+    quarter = owners // 4
+    strip = 2 * quarter
     odd = lax.rem(iota((quarter, LANE), 1) // 4, 2) == 1
-    for part in range(2):
-        mine_too = owner & (tz // 2 == part)
-        from_rows = recv_b.at[pl.ds(owners * part, owners)]
-        but_mine = recv_b.at[pl.ds(owners * part, owners - 2)]
+    for part in range(4):
+        mine_too = tz == part
+        from_rows = recv_b.at[pl.ds(strip * part, strip)]
+        but_mine = recv_b.at[pl.ds(strip * part, strip - 2)]
 
         @pl.when(mine_too)
         def _():
@@ -356,9 +357,9 @@
         def _():
             pltpu.make_async_copy(from_rows, from_rows, b_recv.at[part]).wait()
 
-        paired[part * owners : (part + 1) * owners, :] = recv_b[part * owners : (part + 1) * owners, :].astype(F32)
-        even_row = paired[pl.ds(part * owners, quarter, stride=2), :]
-        odd_row = paired[pl.ds(part * owners + 1, quarter, stride=2), :]
+        paired[part * strip : (part + 1) * strip, :] = recv_b[part * strip : (part + 1) * strip, :].astype(F32)
+        even_row = paired[pl.ds(part * strip, quarter, stride=2), :]
+        odd_row = paired[pl.ds(part * strip + 1, quarter, stride=2), :]
         first = jnp.where(odd, pltpu.roll(odd_row, 4, 1), even_row)
         second = jnp.where(odd, odd_row, pltpu.roll(even_row, LANE - 4, 1))
         flow = jnp.concatenate([first, second], axis=0).T.astype(BF16)
@@ -466,7 +467,7 @@
                 dma,
                 dma,
                 dma,
-                dma((2,)),
+                dma((4,)),
                 dma((n_zone - 1,)),
                 dma((n_zone - 1,)),
                 pltpu.SemaphoreType.REGULAR((4,)),

time: 35.8 us -> 35.7 us (level)
  no operation moved by 1% of the time
where the time goes in v7:
time: 35.7 us; the launch traced here: 35.6 us
  Pallas kernels  35 us (98%)
  local copies, waits for them, and re-layouts  0.63 us (2%)
    pallas_call x1, Pallas kernels, shards(): pl.pallas_call(functools.partial(kernel, n_tm, n_zone), name='flux', out_...  35 us

profile of v7, /device:TPU:1, one launch (start us, length us, event | category | flops | bytes accessed | tf_op | source)
XLA Modules:
  0.0 35.6 jit_solution(8045807888656589681)
XLA Ops:
  0.0 35.0 %flux.1 = f32[8,2048]{1,0:T(8,128)S(1)} custom-call(f32[8,2048]{1,0:T(8,128)} %source.1, bf16[16,8,128,128]{3,2,1,0:T(8,128)(2,1)} %weights.1, s32[8,16]{1,0:T(8,128)} %bitcast.1, s32[1,128]{1,0:T(1,128)} %sizes.1, f32[1023]{0:T(1024)} %taps.1), custom_call_target="tpu_custom_call" | custom-call | tf_op jit(solution)/shard_map/flux/pallas_call | solution.py:437
  35.0 0.6 %copy.7 = f32[8,2048]{1,0:T(8,128)} copy(f32[8,2048]{1,0:T(8,128)S(1)} %flux.1) | data formatting | bytes 131072

commit v8 on v7

--- a/solution.py
+++ b/solution.py
@@ -14,7 +14,7 @@
 LANE = 128
 BLOCKS = 16
 SLOTS = 8
-SLABS = [(0, 1), (2, 3), (4, 5, 6, 7)]
+SLABS = [(0,), (1, 2), (3, 4, 5, 6, 7)]
 BANDS = [(0, 0), (0, 1)] + [(g, u) for g in (1, 2, 3) for u in (0, 1, 2)]
 
 

time: 35.7 us -> 35.7 us (level)
  no operation moved by 1% of the time
where the time goes in v8:
time: 35.7 us; the launch traced here: 35.5 us
  Pallas kernels  34.9 us (98%)
  local copies, waits for them, and re-layouts  0.63 us (2%)
    pallas_call x1, Pallas kernels, shards(): pl.pallas_call(functools.partial(kernel, n_tm, n_zone), name='flux', out_...  34.9 us

profile of v8, /device:TPU:1, one launch (start us, length us, event | category | flops | bytes accessed | tf_op | source)
XLA Modules:
  0.0 35.5 jit_solution(8688986108819612547)
XLA Ops:
  0.0 34.9 %flux.1 = f32[8,2048]{1,0:T(8,128)S(1)} custom-call(f32[8,2048]{1,0:T(8,128)} %source.1, bf16[16,8,128,128]{3,2,1,0:T(8,128)(2,1)} %weights.1, s32[8,16]{1,0:T(8,128)} %bitcast.1, s32[1,128]{1,0:T(1,128)} %sizes.1, f32[1023]{0:T(1024)} %taps.1), custom_call_target="tpu_custom_call" | custom-call | tf_op jit(solution)/shard_map/flux/pallas_call | solution.py:437
  34.9 0.6 %copy.7 = f32[8,2048]{1,0:T(8,128)} copy(f32[8,2048]{1,0:T(8,128)S(1)} %flux.1) | data formatting | bytes 131072
